TPU v7x, 32 devices: a whole 2x2x4 slice. The times are simulated.
32 devices in a mesh: dp: 8 (over z, x), mp: 4 (over y, core).
Axes of the slice: x: 2, y: 2, z: 4, core: 2. Of those that a mesh axis runs over, the one named last changes fastest.
Arguments:
- tokens: bfloat16 [8192, 768], P('dp'), may hold values from -6 to 6
- cotangent: bfloat16 [8192, 768], P('dp'), may hold values from -6 to 6
- lengths: int32 [32], P('dp'), may hold values from 32 to 256, as said below
- w_qkv: bfloat16 [768, 3, 768], P('dp', None, 'mp'), may hold values from -0.21875 to 0.21875
- qv_bias: bfloat16 [2, 4, 192], P(None, 'mp', 'dp'), may hold values from -3 to 3
- w_out: bfloat16 [768, 768], P('mp', 'dp'), may hold values from -1.75 to 1.75
- w_in: bfloat16 [768, 3072], P('dp', 'mp'), may hold values from -0.21875 to 0.21875
- in_bias: bfloat16 [4, 768], P('mp', 'dp'), may hold values from -3 to 3
- w_down: bfloat16 [3072, 768], P('mp', 'dp'), may hold values from -0.109375 to 0.109375
- pilot: bfloat16 [3072, 768], P('mp', 'dp'), may hold values from -0.109375 to 0.109375
- gains: bfloat16 [2, 768], P(None, 'dp'), may hold values from 0.25 to 1.75
- shifts: bfloat16 [4, 768], P(None, 'dp'), may hold values from -3 to 3
Outputs:
- output: bfloat16 [8192, 768], P('dp')
- input_grad: float32 [8192, 768], P('dp')
- along: float32 [8192, 768], P('dp')
- grad_qkv: float32 [768, 3, 768], P('dp', None, 'mp')
- grad_qv_bias: float32 [2, 4, 192], P(None, 'mp', 'dp')
- grad_out: float32 [768, 768], P('mp', 'dp')
- grad_in: float32 [768, 3072], P('dp', 'mp')
- grad_in_bias: float32 [4, 768], P('mp', 'dp')
- grad_down: float32 [3072, 768], P('mp', 'dp')
- grad_gains: float32 [2, 768], P(None, 'dp')
- grad_shifts: float32 [4, 768], P(None, 'dp')
Inputs may be any that keep to these rules, and one draw needn't show every extreme that they name: `lengths`: the number of real tokens of a sequence, the rest of its 256 positions being padding; some sequence is full.
All inputs are finite; a program needn't handle non-finite values.
Results may differ from a plain program's by a relative error of at most 0.02.
Values may be sent and summed in bfloat16 or wider, within the bound.
A program may use at most 128 MiB of HBM per device.

v0:
```python
import jax
import jax.numpy as jnp
from jax import lax
from jax.sharding import PartitionSpec as P

HEAD_DIM = 64
SEQ_LEN = 256
MB = 2
SB = 2


epsilon = 1e-06


def affine_norm(stream, gain, shift):
    centered_input = stream - jnp.mean(stream, -1, keepdims=True)
    return (
        centered_input
        * lax.rsqrt(jnp.mean(centered_input * centered_input, -1, keepdims=True) + epsilon)
        * gain
        + shift
    )


def exact_gelu(values):
    return jax.nn.gelu(values, approximate=False)


def add_trees(first_tree, second_tree):
    return tuple((left + right for left, right in zip(first_tree, second_tree)))


def micro_step(fetched, inputs, upstream, seq_lengths, positions):
    (
        full_qkv,
        full_qvb,
        full_out,
        full_in,
        full_ib,
        full_down,
        full_pilot,
        full_gains,
        full_shifts,
    ) = fetched
    model_width = inputs.shape[1]
    head_cols = full_qkv.shape[2]
    heads_here = head_cols // HEAD_DIM
    batch_rows = inputs.shape[0]
    seq_count = seq_lengths.shape[0]
    score_scale = HEAD_DIM ** (-0.5)
    share = batch_rows // lax.axis_size("mp")
    row_start = lax.axis_index("mp") * share

    def own_rows(values):
        return lax.dynamic_slice_in_dim(values, row_start, share, 0)

    bias_pair = full_qvb.reshape(2, head_cols).astype(jnp.float32)
    hidden_bias = full_ib.reshape(-1).astype(jnp.float32)
    gain_rows = full_gains.astype(jnp.float32)
    shift_rows = full_shifts.astype(jnp.float32)
    qkv_matrix = full_qkv.reshape(model_width, 3 * head_cols)
    bias_rows = jnp.stack([bias_pair[0], jnp.zeros_like(bias_pair[0]), bias_pair[1]])
    projected = jnp.dot(inputs, qkv_matrix, preferred_element_type=jnp.float32).reshape(
        batch_rows, 3, head_cols
    )
    projected = (projected + bias_rows).astype(jnp.bfloat16)
    split_heads = projected.reshape(seq_count, SEQ_LEN, 3, heads_here, HEAD_DIM)
    queries = split_heads[:, :, 0]
    key_matrix_rows = split_heads[:, :, 1]
    value_rows = split_heads[:, :, 2]
    keep = positions[None, :] < seq_lengths[:, None]

    def scores_of():
        raw = (
            jnp.einsum(
                "bqhd,bkhd->bhqk", queries, key_matrix_rows, preferred_element_type=jnp.float32
            )
            * score_scale
        )
        return jnp.where(keep[:, None, None, :], raw, -1000000000.0)

    scores = scores_of()
    top = jnp.max(scores, -1, keepdims=True)
    expo = jnp.exp(scores - top)
    total = jnp.sum(expo, -1, keepdims=True)
    log_total = top + jnp.log(total)
    probs_low = (expo / total).astype(jnp.bfloat16)
    context = jnp.einsum(
        "bhqk,bkhd->bqhd", probs_low, value_rows, preferred_element_type=jnp.float32
    )
    context = context.reshape(batch_rows, head_cols).astype(jnp.bfloat16)
    attended_part = jnp.dot(context, full_out, preferred_element_type=jnp.float32)
    attended = lax.psum_scatter(
        attended_part.astype(jnp.bfloat16), "mp", scatter_dimension=0, tiled=True
    ).astype(jnp.float32)
    opening_residual = own_rows(inputs).astype(jnp.float32) + attended + shift_rows[0]
    normed, norm_back = jax.vjp(affine_norm, opening_residual, gain_rows[0], shift_rows[1])
    normed_low = lax.all_gather(normed.astype(jnp.bfloat16), "mp", axis=0, tiled=True)
    hidden_pre = jnp.dot(normed_low, full_in, preferred_element_type=jnp.float32) + hidden_bias
    hidden_full, gelu_back = jax.vjp(exact_gelu, hidden_pre)
    hidden = hidden_full.astype(jnp.bfloat16)
    branch_part = jnp.dot(hidden, full_down, preferred_element_type=jnp.float32)
    tangent_part = jnp.dot(hidden, full_pilot, preferred_element_type=jnp.float32)
    branch, tangent_total_sum = (
        lax.psum_scatter(
            branch_part.astype(jnp.bfloat16), "mp", scatter_dimension=0, tiled=True
        ).astype(jnp.float32),
        lax.psum_scatter(
            tangent_part.astype(jnp.bfloat16), "mp", scatter_dimension=0, tiled=True
        ).astype(jnp.float32),
    )
    stream = normed + branch + shift_rows[2]
    output, out_back = jax.vjp(affine_norm, stream, gain_rows[1], shift_rows[3])
    centered_input = stream - jnp.mean(stream, -1, keepdims=True)
    inverse_deviation = lax.rsqrt(
        jnp.mean(centered_input * centered_input, -1, keepdims=True) + epsilon
    )
    normalized_input = centered_input * inverse_deviation
    along = (
        gain_rows[1]
        * inverse_deviation
        * (
            tangent_total_sum
            - jnp.mean(tangent_total_sum, -1, keepdims=True)
            - normalized_input * jnp.mean(tangent_total_sum * normalized_input, -1, keepdims=True)
        )
    )
    row_keep = own_rows(keep.reshape(batch_rows, 1).astype(jnp.float32))
    stream_grad, gain_two, shift_four = out_back(own_rows(upstream).astype(jnp.float32) * row_keep)
    branch_low = lax.all_gather(stream_grad.astype(jnp.bfloat16), "mp", axis=0, tiled=True)
    grad_down = jnp.einsum("rf,rd->fd", hidden, branch_low, preferred_element_type=jnp.float32)
    hidden_grad = jnp.einsum("rd,fd->rf", branch_low, full_down, preferred_element_type=jnp.float32)
    (pre_grad,) = gelu_back(hidden_grad)
    pre_low = pre_grad.astype(jnp.bfloat16)
    grad_in = jnp.einsum("rd,rf->df", normed_low, pre_low, preferred_element_type=jnp.float32)
    grad_ib = jnp.sum(pre_low.astype(jnp.float32), 0)
    normed_part = jnp.einsum("rf,df->rd", pre_low, full_in, preferred_element_type=jnp.float32)
    normed_grad = (
        lax.psum_scatter(
            normed_part.astype(jnp.bfloat16), "mp", scatter_dimension=0, tiled=True
        ).astype(jnp.float32)
        + stream_grad
    )
    first_grad, gain_one, shift_two = norm_back(normed_grad)
    attended_low = lax.all_gather(first_grad.astype(jnp.bfloat16), "mp", axis=0, tiled=True)
    grad_out = jnp.einsum("rc,rd->cd", context, attended_low, preferred_element_type=jnp.float32)
    context_grad = jnp.einsum(
        "rd,cd->rc", attended_low, full_out, preferred_element_type=jnp.float32
    )
    context_grad = context_grad.astype(jnp.bfloat16).reshape(
        seq_count, SEQ_LEN, heads_here, HEAD_DIM
    )
    probs = jnp.exp(scores_of() - log_total)
    value_grad = jnp.einsum(
        "bhqk,bqhd->bkhd",
        probs.astype(jnp.bfloat16),
        context_grad,
        preferred_element_type=jnp.float32,
    )
    prob_grad = jnp.einsum(
        "bqhd,bkhd->bhqk", context_grad, value_rows, preferred_element_type=jnp.float32
    )
    score_grad = (probs * (prob_grad - jnp.sum(probs * prob_grad, -1, keepdims=True))).astype(
        jnp.bfloat16
    )
    query_grad = (
        jnp.einsum(
            "bhqk,bkhd->bqhd", score_grad, key_matrix_rows, preferred_element_type=jnp.float32
        )
        * score_scale
    )
    key_grad = (
        jnp.einsum("bhqk,bqhd->bkhd", score_grad, queries, preferred_element_type=jnp.float32)
        * score_scale
    )
    projected_grad = jnp.stack([query_grad, key_grad, value_grad], 2).reshape(
        batch_rows, 3 * head_cols
    )
    projected_grad = projected_grad.astype(jnp.bfloat16)
    grad_qkv = jnp.einsum("rd,rc->dc", inputs, projected_grad, preferred_element_type=jnp.float32)
    grad_qkv = grad_qkv.reshape(model_width, 3, head_cols)
    bias_sums = jnp.sum(projected_grad.astype(jnp.float32), 0).reshape(3, head_cols)
    grad_qvb = jnp.stack([bias_sums[0], bias_sums[2]]).reshape(2, 1, head_cols)
    input_part = jnp.einsum(
        "rc,dc->rd", projected_grad, qkv_matrix, preferred_element_type=jnp.float32
    )
    input_grad = (
        lax.psum_scatter(
            input_part.astype(jnp.bfloat16), "mp", scatter_dimension=0, tiled=True
        ).astype(jnp.float32)
        + first_grad
    )
    norm_terms = jnp.stack(
        [gain_one, gain_two, jnp.sum(first_grad, 0), shift_two, jnp.sum(stream_grad, 0), shift_four]
    )
    output_low = output.astype(jnp.bfloat16)
    whole_out, input_grad, along, norm_parts = (
        lax.all_gather(
            output_low.astype(jnp.float32).astype(jnp.bfloat16), "mp", axis=0, tiled=True
        ).astype(jnp.float32),
        lax.all_gather(input_grad.astype(jnp.bfloat16), "mp", axis=0, tiled=True).astype(
            input_grad.dtype
        ),
        lax.all_gather(along.astype(jnp.bfloat16), "mp", axis=0, tiled=True).astype(along.dtype),
        lax.all_gather(norm_terms[None].astype(jnp.bfloat16), "mp", axis=0, tiled=True).astype(
            jnp.float32
        ),
    )
    output_low = whole_out.astype(jnp.bfloat16)
    norm_terms = jnp.sum(norm_parts, 0)
    grads = (
        grad_qkv,
        grad_qvb,
        grad_out,
        grad_in,
        grad_ib.reshape(1, -1),
        grad_down,
        norm_terms[0:2],
        norm_terms[2:6],
    )
    return ((output_low, input_grad, along), grads)


def local(
    tokens, cotangent, lengths, w_qkv, qv_bias, w_out, w_in, in_bias, w_down, pilot, gains, shifts
):
    batch_rows = SB * SEQ_LEN
    positions = jnp.arange(SEQ_LEN, dtype=jnp.int32)
    totals = None
    settled = None
    results = []
    for batch_index in range(MB):
        fetched = (
            lax.all_gather(w_qkv, "dp", axis=0, tiled=True),
            lax.all_gather(qv_bias, "dp", axis=2, tiled=True),
            lax.all_gather(w_out, "dp", axis=1, tiled=True),
            lax.all_gather(w_in, "dp", axis=0, tiled=True),
            lax.all_gather(in_bias, "dp", axis=1, tiled=True),
            lax.all_gather(w_down, "dp", axis=1, tiled=True),
            lax.all_gather(pilot, "dp", axis=1, tiled=True),
            lax.all_gather(gains, "dp", axis=1, tiled=True),
            lax.all_gather(shifts, "dp", axis=1, tiled=True),
        )
        first_row = batch_index * batch_rows
        inputs = tokens[first_row : first_row + batch_rows]
        upstream = cotangent[first_row : first_row + batch_rows]
        seq_lengths = lengths[batch_index * SB : (batch_index + 1) * SB]
        result, grads = micro_step(fetched, inputs, upstream, seq_lengths, positions)
        results.append(result)
        totals = grads if totals is None else add_trees(totals, grads)
    settled = (
        lax.psum_scatter(totals[0], "dp", scatter_dimension=0, tiled=True),
        lax.psum_scatter(totals[1], "dp", scatter_dimension=2, tiled=True),
        lax.psum_scatter(totals[2], "dp", scatter_dimension=1, tiled=True),
        lax.psum_scatter(totals[3], "dp", scatter_dimension=0, tiled=True),
        lax.psum_scatter(totals[4], "dp", scatter_dimension=1, tiled=True),
        lax.psum_scatter(totals[5], "dp", scatter_dimension=1, tiled=True),
        lax.psum_scatter(totals[6], "dp", scatter_dimension=1, tiled=True),
        lax.psum_scatter(totals[7], "dp", scatter_dimension=1, tiled=True),
    )
    output = jnp.concatenate([item[0] for item in results], 0)
    input_grad = jnp.concatenate([item[1] for item in results], 0)
    along = jnp.concatenate([item[2] for item in results], 0)
    return (output, input_grad, along) + tuple(settled)


def solution(mesh):
    in_specs = (
        P("dp", None),
        P("dp", None),
        P("dp"),
        P("dp", None, "mp"),
        P(None, "mp", "dp"),
        P("mp", "dp"),
        P("dp", "mp"),
        P("mp", "dp"),
        P("mp", "dp"),
        P("mp", "dp"),
        P(None, "dp"),
        P(None, "dp"),
    )
    out_specs = (
        P("dp", None),
        P("dp", None),
        P("dp", None),
        P("dp", None, "mp"),
        P(None, "mp", "dp"),
        P("mp", "dp"),
        P("dp", "mp"),
        P("mp", "dp"),
        P("mp", "dp"),
        P(None, "dp"),
        P(None, "dp"),
    )
    return jax.shard_map(local, mesh=mesh, in_specs=in_specs, out_specs=out_specs, check_vma=False)
```

profile of v0, /device:TPU:25, one launch (start us, length us, event | category | flops | bytes accessed | tf_op | source)
XLA Modules:
  0.0 927.8 jit_solution(13783035590865547423)
XLA Ops:
  10.9 21.7 %all_gather.79 = bf16[2,1,192]{1,0,2:T(2,128)(2,1)S(1)} all-gather(bf16[2,1,24]{1,0,2:T(2,128)(2,1)S(1)} %copy.128), channel_id=1, replica_groups=mesh['dp'=8,'mp'=4] {'dp'}, dimensions={2}, use_global_device_ids=true | all-gather | bytes 864 | tf_op jit(solution)/shard_map/all_gather | solution.py:235
  34.9 25.3 %all_gather.80 = bf16[192,768]{0,1:T(8,128)(2,1)S(1)} all-gather(bf16[192,96]{0,1:T(8,128)(2,1)S(1)} %copy.134), channel_id=1, replica_groups=mesh['dp'=8,'mp'=4] {'dp'}, dimensions={1}, use_global_device_ids=true | all-gather | bytes 331776 | tf_op jit(solution)/shard_map/all_gather | solution.py:236
  60.2 33.6 %all_gather.78 = bf16[768,3,192]{2,1,0:T(4,128)(2,1)S(1)} all-gather(bf16[96,3,192]{2,1,0:T(4,128)(2,1)S(1)} %copy.126), channel_id=1, replica_groups=mesh['dp'=8,'mp'=4] {'dp'}, dimensions={0}, use_global_device_ids=true | all-gather | bytes 995328 | tf_op jit(solution)/shard_map/all_gather | solution.py:234
  102.8 2.6 fusion.15
  113.9 2.6 fusion.78
  118.6 14.5 %all-reduce = bf16[768]{0:T(1024)(128)(2,1)S(1)} all-reduce(bf16[768]{0:T(1024)(128)(2,1)S(1)} %dynamic-update-slice), channel_id=1, replica_groups=mesh['dp'=8,'mp'=4] {'dp'}, use_global_device_ids=true, to_apply=%add | all-reduce | flops 768 | bytes 3072
  133.8 14.7 %all-gather.1 = bf16[8,96,2]{1,2,0:T(2,128)(2,1)S(1)} all-gather(bf16[1,96,2]{1,2,0:T(2,128)(2,1)S(1)} %bitcast.232), channel_id=1, replica_groups=mesh['dp'=8,'mp'=4] {'dp'}, dimensions={0}, use_global_device_ids=true | all-gather | bytes 3456 | tf_op jit(solution)/shard_map/all_gather | solution.py:241
  149.2 12.7 %all-gather = bf16[8,96,4]{1,2,0:T(4,128)(2,1)S(1)} all-gather(bf16[1,96,4]{1,2,0:T(4,128)(2,1)S(1)} %bitcast.231), channel_id=1, replica_groups=mesh['dp'=8,'mp'=4] {'dp'}, dimensions={0}, use_global_device_ids=true | all-gather | bytes 6912 | tf_op jit(solution)/shard_map/all_gather | solution.py:242
  165.8 8.0 reduce-scatter.31.cloned.1.call-done
  179.7 32.0 %all_gather.88 = bf16[512,768]{1,0:T(8,128)(2,1)} all-gather(bf16[128,768]{1,0:T(8,128)(2,1)S(1)} %get-tuple-element.92), channel_id=1, replica_groups=mesh['dp'=8,'mp'=4] {'mp'}, dimensions={0}, use_global_device_ids=true | all-gather | bytes 983040 | tf_op jit(solution)/shard_map/all_gather | solution.py:98
  211.7 7.3 multiply_convert_fusion.2
  219.0 3.3 convolution_convert_fusion.4
  222.4 8.9 all_gather.83
  231.3 6.7 multiply_convert_fusion.3
  240.7 17.3 %all-gather.10.cloned.1.call-done = bf16[768,768]{0,1:T(8,128)(2,1)} async-done(((bf16[768,96]{0,1:T(8,128)(2,1)}), bf16[768,768]{0,1:T(8,128)(2,1)}) %all-gather.10.cloned.1.call-update) | async-done | bytes 1179664 | tf_op jit(solution)/shard_map/all_gather | solution.py:240
  258.1 3.2 convolution_convert_fusion.1
  263.8 2.8 fusion.77
  268.4 3.1 reduce-scatter.29.cloned.1.call-done
  276.1 21.1 %reduce-scatter.43.cloned.1.call-done = bf16[128,768]{1,0:T(8,128)(2,1)} async-done(((bf16[512,768]{1,0:T(8,128)(2,1)}), bf16[128,768]{1,0:T(8,128)(2,1)}) %reduce-scatter.43.cloned.1.call-update) | async-done | bytes 196624 | tf_op jit(solution)/shard_map/reduce_scatter | solution.py:108
  302.9 20.0 %reduce-scatter.45.cloned.1.call-done = bf16[128,768]{1,0:T(8,128)(2,1)} async-done(((bf16[512,768]{1,0:T(8,128)(2,1)}), bf16[128,768]{1,0:T(8,128)(2,1)}) %reduce-scatter.45.cloned.1.call-update) | async-done | bytes 196624 | tf_op jit(solution)/shard_map/reduce_scatter | solution.py:108
  322.9 3.4 fusion.34
  328.0 8.9 all_gather.90
  337.0 3.5 convert_reduce_fusion.1
  343.1 2.4 fusion.38
  346.4 8.7 all_gather.93
  355.1 3.5 convert_reduce_fusion
  370.1 22.6 %reduce-scatter.39.cloned.1.call-done = bf16[128,768]{1,0:T(8,128)(2,1)} async-done(((bf16[512,768]{1,0:T(8,128)(2,1)}), bf16[128,768]{1,0:T(8,128)(2,1)}) %reduce-scatter.39.cloned.1.call-update) | async-done | bytes 196624 | tf_op jit(solution)/shard_map/reduce_scatter | solution.py:139
  404.0 6.1 all_gather.100
  414.4 5.5 all_gather.99
  420.0 8.9 all_gather.91
  431.8 9.1 all_gather.94
  445.8 2.6 convolution_add_fusion.7
  451.2 2.2 copy.165
  473.3 2.3 convolution_add_fusion
  481.7 8.7 all_gather.89
  490.4 8.7 all_gather.87
  500.4 8.7 all_gather.98
  509.1 8.7 all_gather.97
  521.4 13.1 %all-reduce.1 = f32[2,1,192]{2,1,0:T(1,128)S(1)} all-reduce(f32[2,1,192]{2,1,0:T(1,128)S(1)} %maximum_add_fusion), channel_id=13, replica_groups=mesh['dp'=8,'mp'=4] {'dp'}, use_global_device_ids=true, to_apply=%region_39.40.clone | all-reduce | flops 384 | bytes 3072
  536.5 47.4 %reduce-scatter.59.cloned.1.call-done = f32[96,4]{1,0:T(8,128)} async-done(((f32[768,4]{1,0:T(8,128)}), f32[96,4]{1,0:T(8,128)}) %reduce-scatter.59.cloned.1.call-update) | async-done | bytes 1552
  585.4 64.3 %reduce-scatter.53.cloned.1.call-done = f32[96,192]{1,0:T(8,128)} async-done(((f32[768,192]{1,0:T(8,128)}), f32[96,192]{1,0:T(8,128)}) %reduce-scatter.53.cloned.1.call-update) | async-done | bytes 73744
  651.3 26.6 %reduce-scatter.41.cloned.1.call-done = bf16[128,768]{1,0:T(8,128)(2,1)} async-done(((bf16[512,768]{1,0:T(8,128)(2,1)}), bf16[128,768]{1,0:T(8,128)(2,1)}) %reduce-scatter.41.cloned.1.call-update) | async-done | bytes 196624 | tf_op jit(solution)/shard_map/reduce_scatter | solution.py:188
  678.9 24.6 %reduce-scatter.37.cloned.1.call-done = bf16[128,768]{1,0:T(8,128)(2,1)} async-done(((bf16[512,768]{1,0:T(8,128)(2,1)}), bf16[128,768]{1,0:T(8,128)(2,1)}) %reduce-scatter.37.cloned.1.call-update) | async-done | bytes 196624 | tf_op jit(solution)/shard_map/reduce_scatter | solution.py:188
  704.6 8.7 all_gather.95
  713.3 8.7 all_gather.92
  723.8 50.6 %reduce-scatter.49.cloned.1.call-done = f32[96,768]{1,0:T(8,128)} async-done(((f32[768,768]{1,0:T(8,128)}), f32[96,768]{1,0:T(8,128)}) %reduce-scatter.49.cloned.1.call-update) | async-done | bytes 294928 | tf_op jit(solution)/shard_map/reduce_scatter | solution.py:255
  774.4 72.7 %reduce-scatter.51.cloned.1.call-done = f32[768,96]{0,1:T(8,128)} async-done(((f32[768,768]{0,1:T(8,128)}), f32[768,96]{0,1:T(8,128)}) %reduce-scatter.51.cloned.1.call-update) | async-done | bytes 294928 | tf_op jit(solution)/shard_map/reduce_scatter | solution.py:257
  847.2 72.8 %reduce-scatter.47.cloned.1.call-done = f32[96,3,192]{2,0,1:T(8,128)} async-done(((f32[768,3,192]{2,0,1:T(8,128)}), f32[96,3,192]{2,0,1:T(8,128)}) %reduce-scatter.47.cloned.1.call-update) | async-done | bytes 221200 | tf_op jit(solution)/shard_map/reduce_scatter | solution.py:252
  (392 shorter events, 133.5 us)
Async XLA Ops:
  8.0 156.1 %reduce-scatter.27.cloned.1.call-start = ((), (), s32[]{:S(2)}) async-start(), calls=%async_computation.17 | async-start | bytes 983040 | tf_op jit(solution)/shard_map/reduce_scatter | solution.py:93
  102.7 71.0 %reduce-scatter.31.cloned.1.call-start = ((), (), s32[]{:S(2)}) async-start(), calls=%async_computation.21 | async-start | bytes 983040 | tf_op jit(solution)/shard_map/reduce_scatter | solution.py:93
  112.0 99.7 %all-gather.6.cloned.1.call-start = ((), (), s32[]{:S(2)}) async-start(), calls=%async_computation.18 | async-start | bytes 1327104 | tf_op jit(solution)/shard_map/all_gather | solution.py:237
  112.6 106.4 %all-gather.8.cloned.1.call-start = ((), (), s32[]{:S(2)}) async-start(), calls=%async_computation.19 | async-start | bytes 1327104 | tf_op jit(solution)/shard_map/all_gather | solution.py:239
  113.2 144.8 %all-gather.10.cloned.1.call-start = ((), (), s32[]{:S(2)}) async-start(), calls=%async_computation.27 | async-start | bytes 1327104 | tf_op jit(solution)/shard_map/all_gather | solution.py:240
  113.8 154.6 %reduce-scatter.33.cloned.1.call-start = ((), (), s32[]{:S(2)}) async-start(), calls=%async_computation.22 | async-start | bytes 983040 | tf_op jit(solution)/shard_map/reduce_scatter | solution.py:105
  113.9 19.9 %copy-start.89 = (bf16[2,96]{1,0:T(2,128)(2,1)S(1)}, bf16[2,96]{1,0:T(2,128)(2,1)}, u32[]{:S(2)}) copy-start(bf16[2,96]{1,0:T(2,128)(2,1)} %param.22) | copy-start | bytes 1156
  113.9 35.3 %copy-start.82 = (bf16[4,96]{1,0:T(4,128)(2,1)S(1)}, bf16[4,96]{1,0:T(4,128)(2,1)}, u32[]{:S(2)}) copy-start(bf16[4,96]{1,0:T(4,128)(2,1)} %param.23) | copy-start | bytes 2308
  222.3 49.2 %reduce-scatter.29.cloned.1.call-start = ((), (), s32[]{:S(2)}) async-start(), calls=%async_computation.20 | async-start | bytes 983040 | tf_op jit(solution)/shard_map/reduce_scatter | solution.py:105
  231.3 6.7 copy-start.13
  231.3 7.6 copy-start.92
  240.7 56.5 %reduce-scatter.43.cloned.1.call-start = ((), (), s32[]{:S(2)}) async-start(), calls=%async_computation.28 | async-start | bytes 983040 | tf_op jit(solution)/shard_map/reduce_scatter | solution.py:108
  261.3 61.6 %reduce-scatter.45.cloned.1.call-start = ((), (), s32[]{:S(2)}) async-start(), calls=%async_computation.29 | async-start | bytes 983040 | tf_op jit(solution)/shard_map/reduce_scatter | solution.py:108
  268.4 101.7 %reduce-scatter.35.cloned.1.call-start = ((), (), s32[]{:S(2)}) async-start(), calls=%async_computation.23 | async-start | bytes 983040 | tf_op jit(solution)/shard_map/reduce_scatter | solution.py:139
  322.9 14.1 %copy-start.93 = (bf16[768,768]{0,1:T(8,128)(2,1)S(1)}, bf16[768,768]{0,1:T(8,128)(2,1)}, u32[]{:S(2)}) copy-start(bf16[768,768]{0,1:T(8,128)(2,1)} %all-gather.8.cloned.1.call-done) | copy-start | bytes 3538948
  322.9 14.1 %copy-start.97 = (f32[512,768]{1,0:T(8,128)S(1)}, f32[512,768]{1,0:T(8,128)}, u32[]{:S(2)}) copy-start(f32[512,768]{1,0:T(8,128)} %get-tuple-element.62) | copy-start | bytes 4718596
  326.9 10.0 %copy-start.72 = (f32[128]{0:T(128)}, f32[128]{0:T(128)S(1)}, u32[]{:S(2)}) copy-start(f32[128]{0:T(128)S(1)} %negate_multiply_fusion.5) | copy-start | bytes 1540
  337.0 4.4 copy-start.90
  343.1 49.6 %reduce-scatter.39.cloned.1.call-start = ((), (), s32[]{:S(2)}) async-start(), calls=%async_computation.25 | async-start | bytes 983040 | tf_op jit(solution)/shard_map/reduce_scatter | solution.py:139
  343.1 12.0 %copy-start.94 = (bf16[768,768]{0,1:T(8,128)(2,1)S(1)}, bf16[768,768]{0,1:T(8,128)(2,1)}, u32[]{:S(2)}) copy-start(bf16[768,768]{0,1:T(8,128)(2,1)} %all-gather.8.cloned.1.call-done) | copy-start | bytes 3538948
  343.1 12.0 %copy-start.96 = (f32[512,768]{1,0:T(8,128)S(1)}, f32[512,768]{1,0:T(8,128)}, u32[]{:S(2)}) copy-start(f32[512,768]{1,0:T(8,128)} %get-tuple-element.66) | copy-start | bytes 4718596
  345.6 9.5 %copy-start.74 = (f32[128]{0:T(128)}, f32[128]{0:T(128)S(1)}, u32[]{:S(2)}) copy-start(f32[128]{0:T(128)S(1)} %negate_multiply_fusion.3) | copy-start | bytes 1540
  355.1 4.4 copy-start.91
  361.2 158.4 %reduce-scatter.55.cloned.1.call-start = ((), (), s32[]{:S(2)}) async-start(), calls=%async_computation.34 | async-start | bytes 442368
  370.0 165.1 %reduce-scatter.57.cloned.1.call-start = ((), (), s32[]{:S(2)}) async-start(), calls=%async_computation.35 | async-start | bytes 442368
  392.7 4.8 copy-start.84
  392.7 4.8 copy-start.1
  392.8 4.8 copy-start.12
  392.8 4.8 copy-start.50
  392.8 4.8 copy-start.65
  392.8 4.8 copy-start.68
  392.8 4.8 copy-start.75
  414.4 17.4 %copy-start.55 = (bf16[128,768]{1,0:T(8,128)(2,1)S(1)}, bf16[128,768]{1,0:T(8,128)(2,1)}, u32[]{:S(2)}) copy-start(bf16[128,768]{1,0:T(8,128)(2,1)} %get-tuple-element.88) | copy-start | bytes 589828
  420.0 21.0 %copy-start.59 = (f32[6,768]{1,0:T(8,128)}, f32[6,768]{1,0:T(8,128)S(1)}, u32[]{:S(2)}) copy-start(f32[6,768]{1,0:T(8,128)S(1)} %convert_reduce_fusion.7) | copy-start | bytes 55300
  442.7 141.3 %reduce-scatter.59.cloned.1.call-start = ((), (), s32[]{:S(2)}) async-start(), calls=%async_computation.36 | async-start | bytes 442368
  445.8 203.9 %reduce-scatter.53.cloned.1.call-start = ((), (), s32[]{:S(2)}) async-start(), calls=%async_computation.33 | async-start | bytes 884736
  449.5 4.0 copy-start.58
  453.5 224.4 %reduce-scatter.41.cloned.1.call-start = ((), (), s32[]{:S(2)}) async-start(), calls=%async_computation.26 | async-start | bytes 983040 | tf_op jit(solution)/shard_map/reduce_scatter | solution.py:188
  460.7 242.8 %reduce-scatter.37.cloned.1.call-start = ((), (), s32[]{:S(2)}) async-start(), calls=%async_computation.24 | async-start | bytes 983040 | tf_op jit(solution)/shard_map/reduce_scatter | solution.py:188
  467.5 307.0 %reduce-scatter.49.cloned.1.call-start = ((), (), s32[]{:S(2)}) async-start(), calls=%async_computation.31 | async-start | bytes 2654208 | tf_op jit(solution)/shard_map/reduce_scatter | solution.py:255
  471.1 376.0 %reduce-scatter.51.cloned.1.call-start = ((), (), s32[]{:S(2)}) async-start(), calls=%async_computation.32 | async-start | bytes 2654208 | tf_op jit(solution)/shard_map/reduce_scatter | solution.py:257
  475.6 444.4 %reduce-scatter.47.cloned.1.call-start = ((), (), s32[]{:S(2)}) async-start(), calls=%async_computation.30 | async-start | bytes 2654208 | tf_op jit(solution)/shard_map/reduce_scatter | solution.py:252
  480.8 9.6 %copy-start.52 = (bf16[128,768]{1,0:T(8,128)(2,1)S(1)}, bf16[128,768]{1,0:T(8,128)(2,1)}, u32[]{:S(2)}) copy-start(bf16[128,768]{1,0:T(8,128)(2,1)} %get-tuple-element.78) | copy-start | bytes 589828
  499.1 9.9 %copy-start.51 = (bf16[128,768]{1,0:T(8,128)(2,1)S(1)}, bf16[128,768]{1,0:T(8,128)(2,1)}, u32[]{:S(2)}) copy-start(bf16[128,768]{1,0:T(8,128)(2,1)} %get-tuple-element.77) | copy-start | bytes 589828
  517.7 160.1 %copy-start.17 = (f32[128,768]{1,0:T(8,128)S(1)}, f32[128,768]{1,0:T(8,128)}, u32[]{:S(2)}) copy-start(f32[128,768]{1,0:T(8,128)} %copy-done.16) | copy-start | bytes 1179652
  517.7 160.1 %copy-start.81 = (f32[128]{0:T(128)S(1)}, f32[128]{0:T(128)}, u32[]{:S(2)}) copy-start(f32[128]{0:T(128)} %copy-done.80) | copy-start | bytes 1540
  517.8 185.8 %copy-start.15 = (f32[128,768]{1,0:T(8,128)S(1)}, f32[128,768]{1,0:T(8,128)}, u32[]{:S(2)}) copy-start(f32[128,768]{1,0:T(8,128)} %get-tuple-element.52) | copy-start | bytes 1179652
  517.8 185.8 %copy-start.79 = (f32[128]{0:T(128)S(1)}, f32[128]{0:T(128)}, u32[]{:S(2)}) copy-start(f32[128]{0:T(128)} %negate_multiply_fusion.4) | copy-start | bytes 1540
  (70 other events, 111.8 us)
Sparse Core Ops, SparseCore 0:
  102.9 44.4 reduce-scatter.26
  150.5 23.2 reduce-scatter.30
  222.4 23.4 reduce-scatter.32
  248.3 23.2 reduce-scatter.28
  273.9 23.2 reduce-scatter.42
  299.6 23.2 reduce-scatter.44
  343.2 23.1 reduce-scatter.34
  369.5 23.1 reduce-scatter.38
  396.0 59.0 reduce-scatter.54
  458.2 61.1 reduce-scatter.56
  522.7 61.2 reduce-scatter.58
  587.1 62.5 reduce-scatter.52
  652.8 25.0 reduce-scatter.40
  680.3 23.1 reduce-scatter.36
  707.4 66.9 reduce-scatter.48
  778.4 68.7 reduce-scatter.50
  851.1 68.8 reduce-scatter.46
Sparse Core Ops, SparseCore 1:
  114.7 59.5 all-gather.5
  176.4 39.8 all-gather.7
  218.3 39.7 all-gather.9
where the time goes:
time: 942 us; the launch traced here: 928 us
  waiting for transfers between devices  453 us (48%)
  blocking collectives  276 us (29%)
  local copies, waits for them, and re-layouts  68.1 us (7%)
  matrix products  63.8 us (7%)
  other arithmetic  47.2 us (5%)
  between operations  18.6 us (2%)
    unnamed x24, waiting for transfers between devices  114 us
    reduce_scatter x1, waiting for transfers between devices, local(): lax.psum_scatter(totals[0], 'dp', scatter_dimension=0, tiled=True)  72.8 us
    reduce_scatter x1, waiting for transfers between devices, local(): lax.psum_scatter(totals[5], 'dp', scatter_dimension=1, tiled=True)  72.7 us
    reduce_scatter x2, waiting for transfers between devices, micro_step(): lax.psum_scatter(input_part.astype(jnp.bfloat16), 'mp', scatter_dimension...  51.1 us
    reduce_scatter x1, waiting for transfers between devices, local(): lax.psum_scatter(totals[3], 'dp', scatter_dimension=0, tiled=True)  50.6 us
    reduce_scatter x2, waiting for transfers between devices, micro_step(): lax.psum_scatter(tangent_part.astype(jnp.bfloat16), 'mp', scatter_dimensi...  41.1 us
    all_gather x2, blocking collectives, micro_step(): lax.all_gather(normed.astype(jnp.bfloat16), 'mp', axis=0, tiled=True)  40.9 us
    unnamed x217, local copies, waits for them, and re-layouts  34.3 us
  transfers between devices with their start and end apart: 20, of which 13 were waited for; matrix products, arithmetic and copies ran while one was open for 15% of the time, Pallas kernels for 0%

commit v1 on v0

v1 whole, which is shorter than its diff:
```python
import functools
import math

import jax
import jax.numpy as jnp
from jax import lax
from jax.experimental import pallas as pl
from jax.experimental.pallas import tpu as pltpu
from jax.sharding import PartitionSpec as P

HEAD_DIM = 64
SEQ_LEN = 256
EPSILON = 1e-06
NZ, NX, NY, NC = 4, 2, 2, 2
BLOCKS = NZ * NX
GROUP = NY * NC
SMALL_ROWS = 16
BIAS_ROW = 6
QKV_ROW = BIAS_ROW + GROUP
FWD_ROWS = 48
BWD_ROWS = 48
F32 = jnp.float32
BF16 = jnp.bfloat16
QKV, IN, DOWN, PILOT = range(4)


def nt(a, b):
    return lax.dot_general(a, b, (((1,), (1,)), ((), ())), preferred_element_type=F32)


def tn(a, b):
    return lax.dot_general(a, b, (((0,), (0,)), ((), ())), preferred_element_type=F32)


def nn(a, b):
    return jnp.dot(a, b, preferred_element_type=F32)


def row_mean(v):
    return jnp.mean(v, -1, keepdims=True)


def col_sum(v):
    return jnp.sum(v, 0, keepdims=True)


def layer_kernel(
    inner,
    lens,
    tok,
    cot,
    shard_a,
    shard_i,
    shard_d,
    shard_p,
    small,
    out_o,
    along_o,
    ig_o,
    grad_a,
    grad_i,
    grad_d,
    small_sum,
    w_a,
    w_i,
    w_d,
    w_p,
    g_i,
    g_d,
    r_core,
    r_yf,
    r_xf,
    r_xs,
    r_ys,
    r_z,
    par,
    par_in,
    gs,
    gs_in,
    xs,
    cots,
    qkv,
    prob,
    ctx,
    acc,
    xh1,
    rs1,
    low,
    low_t,
    hid,
    gder,
    xh2,
    rs2,
    sgrad,
    bl,
    bl_t,
    qg,
    own,
    s_load,
    s_z,
    r_zs,
    s_x,
    r_x,
    s_y,
    r_y,
    s_dx,
    r_dx,
    s_dy,
    r_dy,
    s_c,
    r_c,
    s_rc,
    r_rc,
    s_red,
    r_red,
    s_rz,
    r_rz,
    s_sm,
    r_sm,
    s_out,
    r_out,
    s_own,
):
    weights = (w_a, w_i, w_d, w_p)
    shards = (shard_a, shard_i, shard_d, shard_p)
    width = xs.shape[1]
    block = w_a.shape[3]
    head_cols = ctx.shape[2]
    qkv_cols = 3 * head_cols
    heads_here = head_cols // HEAD_DIM
    rows = xs.shape[0]
    scale = HEAD_DIM ** (-0.5)

    dp = lax.axis_index("dp")
    mp = lax.axis_index("mp")
    spot = dp // inner
    rest = dp - spot * inner
    z, x = spot // NX, spot % NX
    y, c = mp // NC, mp % NC
    far_y, far_x, far_c = 1 - y, 1 - x, 1 - c
    mine = mp
    over_y = far_y * NC + c
    x_peer = {"dp": (z * NX + far_x) * inner + rest, "mp": mp}
    y_peer = {"dp": dp, "mp": over_y}
    c_peer = {"dp": dp, "mp": y * NC + far_c}

    def z_at(step):
        return (z + step) % NZ

    def z_from(step):
        return (z + NZ - step) % NZ

    def z_peer(step):
        return {"dp": (z_at(step) * NX + x) * inner + rest, "mp": mp}

    sends = []

    def remote(src, dst, send, recv, peer):
        return pltpu.make_async_remote_copy(
            src_ref=src,
            dst_ref=dst,
            send_sem=send,
            recv_sem=recv,
            device_id=peer,
            device_id_type=pl.DeviceIdType.MESH,
        )

    def push(src, dst, send, recv, peer, chunk=None):
        copy = remote(src, dst, send, recv, peer)
        copy.start()
        sends.append((chunk, copy))

    def arrived(dst, send, recv):
        remote(dst, dst, send, recv, c_peer).wait_recv()

    barrier = pltpu.get_barrier_semaphore()
    peers = [x_peer, y_peer, c_peer] + [z_peer(step) for step in range(1, NZ)]
    for peer in peers:
        pl.semaphore_signal(barrier, inc=1, device_id=peer, device_id_type=pl.DeviceIdType.MESH)
    pl.semaphore_wait(barrier, len(peers))

    loads = []
    for k in range(4):
        loads.append(
            pltpu.make_async_copy(shards[k], weights[k].at[mine, z, x], s_load.at[k])
        )
    my_rows = pl.ds(mp * rows, rows)
    loads.append(pltpu.make_async_copy(tok.at[my_rows], xs, s_load.at[4]))
    loads.append(pltpu.make_async_copy(cot.at[my_rows], cots, s_load.at[5]))

    def send_z(k):
        for step in range(1, NZ):
            push(
                shards[k],
                weights[k].at[mine, z, x],
                s_z.at[k, step],
                r_zs.at[k, step],
                z_peer(step),
                k,
            )

    def send_own(k):
        for sem_s, sem_r, peer in ((s_x, r_x, x_peer), (s_y, r_y, y_peer)):
            push(shards[k], weights[k].at[mine, z, x], sem_s.at[k, 0], sem_r.at[k, 0], peer, k)

    def forward_z(k, step):
        src = weights[k].at[mine, z_from(step), x]
        arrived(src, s_z.at[k, step], r_zs.at[k, step])
        push(src, src, s_x.at[k, step], r_x.at[k, step], x_peer, k)
        push(src, src, s_y.at[k, step], r_y.at[k, step], y_peer, k)

    first = pl.ds(0, FWD_ROWS)
    second = pl.ds(FWD_ROWS, block - FWD_ROWS)

    def forward_diagonal(k, step):
        from_x = weights[k].at[mine, z_from(step), far_x]
        arrived(from_x, s_x.at[k, step], r_x.at[k, step])
        part = weights[k].at[mine, z_from(step), far_x, first]
        push(part, part, s_dy.at[k, step], r_dy.at[k, step], y_peer, k)
        from_y = weights[k].at[over_y, z_from(step), x]
        arrived(from_y, s_y.at[k, step], r_y.at[k, step])
        part = weights[k].at[over_y, z_from(step), x, second]
        push(part, part, s_dx.at[k, step], r_dx.at[k, step], x_peer, k)

    def to_core(k, index, block_index, column):
        src = weights[k].at[block_index, :, column]
        push(src, src, s_c.at[k, index], r_c.at[k, index], c_peer, k)

    def finish(k):
        for step in range(NZ):
            arrived(
                weights[k].at[over_y, z_from(step), far_x, first],
                s_dy.at[k, step],
                r_dy.at[k, step],
            )
            arrived(
                weights[k].at[over_y, z_from(step), far_x, second],
                s_dx.at[k, step],
                r_dx.at[k, step],
            )
        to_core(k, 3, over_y, far_x)
        for index, (block_index, column) in enumerate(
            (
                (y * NC + far_c, x),
                (y * NC + far_c, far_x),
                (far_y * NC + far_c, x),
                (far_y * NC + far_c, far_x),
            )
        ):
            arrived(
                weights[k].at[block_index, :, column], s_c.at[k, index], r_c.at[k, index]
            )

    def small_stage(which, buf, buf_in, stage):
        if stage < 3:
            peer = (c_peer, y_peer, x_peer)[stage]
            push(buf.at[stage], buf_in.at[stage], s_sm.at[which, stage], r_sm.at[which, stage], peer)
        else:
            for step in range(1, NZ):
                push(
                    buf.at[3],
                    buf_in.at[2 + step],
                    s_sm.at[which, 2 + step],
                    r_sm.at[which, 2 + step],
                    z_peer(step),
                )

    def small_add(which, buf, buf_in, stage):
        arrived(buf_in.at[stage], s_sm.at[which, stage], r_sm.at[which, stage])
        buf[stage + 1] = buf[stage] + buf_in[stage]

    def small_last(which, buf, buf_in):
        for step in range(1, NZ):
            arrived(buf_in.at[2 + step], s_sm.at[which, 2 + step], r_sm.at[which, 2 + step])
        total = jnp.zeros(buf.shape[1:], F32)
        for place in range(NZ):
            term = buf[3]
            for step in range(1, NZ):
                term = jnp.where(z_from(step) == place, buf_in[2 + step], term)
            total = total + term
        return total

    load_small = pltpu.make_async_copy(small, par.at[0], s_load.at[6])
    load_small.start()
    send_z(QKV)
    for copy in loads:
        copy.start()
    send_own(QKV)
    load_small.wait()
    small_stage(0, par, par_in, 0)
    send_z(IN)
    small_add(0, par, par_in, 0)
    small_stage(0, par, par_in, 1)
    forward_z(QKV, 1)
    small_add(0, par, par_in, 1)
    small_stage(0, par, par_in, 2)
    forward_z(QKV, 3)
    small_add(0, par, par_in, 2)
    small_stage(0, par, par_in, 3)
    forward_z(QKV, 2)
    send_z(DOWN)
    send_z(PILOT)
    for copy in loads:
        copy.wait()
    to_core(QKV, 0, mine, x)
    send_own(IN)
    for step in range(NZ):
        forward_diagonal(QKV, step)
    to_core(QKV, 1, mine, far_x)
    to_core(QKV, 2, over_y, x)
    par[4] = small_last(0, par, par_in)
    for step in (1, 3, 2):
        forward_z(IN, step)
    to_core(IN, 0, mine, x)
    finish(QKV)

    length = lens[mp]
    key_keep = lax.broadcasted_iota(jnp.int32, (rows, rows), 1) < length
    row_keep = (lax.broadcasted_iota(jnp.int32, (rows, 1), 0) < length).astype(F32)

    def par_row(index):
        return par[4, index : index + 1, :]

    def square(ref, m, start, stop):
        value = ref[m, :, :, :, start:stop]
        return value.reshape(width, stop - start)

    def project(m, carry):
        bias = par[4, pl.ds(QKV_ROW + m, 1), :qkv_cols]
        qkv[m] = (nn(xs[...], square(w_a, m, 0, qkv_cols)) + bias).astype(BF16)
        return carry

    lax.fori_loop(0, GROUP, project, 0)

    def attend(m, carry):
        part = qkv[m]
        for h in range(heads_here):
            lo = h * HEAD_DIM
            q = part[:, lo : lo + HEAD_DIM]
            k = part[:, head_cols + lo : head_cols + lo + HEAD_DIM]
            v = part[:, 2 * head_cols + lo : 2 * head_cols + lo + HEAD_DIM]
            score = jnp.where(key_keep, nt(q, k) * scale, -1000000000.0)
            expo = jnp.exp(score - jnp.max(score, -1, keepdims=True))
            weight = expo / jnp.sum(expo, -1, keepdims=True)
            prob[m * heads_here + h] = weight
            ctx[m, :, lo : lo + HEAD_DIM] = nn(weight.astype(BF16), v).astype(BF16)
        return carry

    for step in range(NZ):
        forward_diagonal(IN, step)
    to_core(IN, 1, mine, far_x)
    to_core(IN, 2, over_y, x)
    send_own(DOWN)
    lax.fori_loop(0, GROUP, attend, 0)
    for step in (1, 3, 2):
        forward_z(DOWN, step)
    to_core(DOWN, 0, mine, x)

    acc[...] = jnp.zeros_like(acc)

    def attended(m, carry):
        acc[...] += nt(ctx[m], square(w_a, m, qkv_cols, width))
        return carry

    lax.fori_loop(0, GROUP, attended, 0)
    opening = xs[...].astype(F32) + acc[...] + par_row(2)
    centered = opening - row_mean(opening)
    rstd = lax.rsqrt(row_mean(centered * centered) + EPSILON)
    rs1[...] = rstd
    xhat = centered * rstd
    xh1[...] = xhat
    normed_low = (xhat * par_row(0) + par_row(3)).astype(BF16)
    low[...] = normed_low
    finish(IN)
    for step in range(NZ):
        forward_diagonal(DOWN, step)
    to_core(DOWN, 1, mine, far_x)
    to_core(DOWN, 2, over_y, x)
    send_own(PILOT)

    def expand(m, carry):
        pre = nn(low[...], square(w_i, m, 0, width)) + par[4, pl.ds(BIAS_ROW + m, 1), :]
        gate = 0.5 + 0.5 * lax.erf(pre * math.sqrt(0.5))
        hid[m] = (pre * gate).astype(BF16)
        gder[m] = gate + pre * (jnp.exp(-0.5 * pre * pre) * (1.0 / math.sqrt(2.0 * math.pi)))
        return carry

    lax.fori_loop(0, GROUP, expand, 0)
    low_t[...] = low[...].T
    for step in (1, 3, 2):
        forward_z(PILOT, step)
    to_core(PILOT, 0, mine, x)
    finish(DOWN)

    acc[...] = xh1[...] * par_row(0) + par_row(3) + par_row(4)

    def contract(m, carry):
        acc[...] += nt(hid[m], square(w_d, m, 0, width))
        return carry

    lax.fori_loop(0, GROUP, contract, 0)
    for step in range(NZ):
        forward_diagonal(PILOT, step)
    to_core(PILOT, 1, mine, far_x)
    to_core(PILOT, 2, over_y, x)

    stream = acc[...]
    centered = stream - row_mean(stream)
    rstd = lax.rsqrt(row_mean(centered * centered) + EPSILON)
    rs2[...] = rstd
    xhat = centered * rstd
    xh2[...] = xhat
    own[0] = (xhat * par_row(1) + par_row(5)).astype(BF16)

    outs = (out_o, along_o, ig_o)

    def send_result(index):
        dst = outs[index].at[my_rows]
        pltpu.make_async_copy(own.at[index], dst, s_own.at[index]).start()
        push(own.at[index], dst, s_out.at[index, 0], r_out.at[index, 0], y_peer)
        push(own.at[index], dst, s_out.at[index, 1], r_out.at[index, 1], c_peer)

    def forward_result(index):
        part = outs[index].at[pl.ds(over_y * rows, rows)]
        arrived(part, s_out.at[index, 0], r_out.at[index, 0])
        push(part, part, s_out.at[index, 2], r_out.at[index, 2], c_peer)

    def finish_result(index):
        pltpu.make_async_copy(own.at[index], outs[index].at[my_rows], s_own.at[index]).wait()
        near = outs[index].at[pl.ds((y * NC + far_c) * rows, rows)]
        arrived(near, s_out.at[index, 1], r_out.at[index, 1])
        far = outs[index].at[pl.ds((far_y * NC + far_c) * rows, rows)]
        arrived(far, s_out.at[index, 2], r_out.at[index, 2])

    send_result(0)

    gs[0] = jnp.zeros(gs.shape[1:], F32)

    def norm_back(grad, xhat, rstd, gain):
        hat = grad * gain
        return rstd * (hat - row_mean(hat) - xhat * row_mean(hat * xhat))

    masked = cots[...].astype(F32) * row_keep
    xhat = xh2[...]
    gs[0, 1:2, :] = col_sum(masked * xhat)
    gs[0, 5:6, :] = col_sum(masked)
    stream_grad = norm_back(masked, xhat, rs2[...], par_row(1))
    gs[0, 4:5, :] = col_sum(stream_grad)
    sgrad[...] = stream_grad
    bl[...] = stream_grad.astype(BF16)
    bl_t[...] = bl[...].T
    acc[...] = stream_grad

    def block_of(i):
        other = i < NY
        return jnp.where(other, i * NC + far_c, (i - NY) * NC + c)

    slab = NX * block

    def outer(left_t, right, ref, m, start, stop):
        def one(zz, carry):
            top = pl.multiple_of(zz * slab, slab)
            value = nn(left_t[pl.ds(top, slab), :], right[...])
            ref[m, zz, :, :, start:stop] = value.astype(BF16).reshape(NX, block, stop - start)
            return carry

        lax.fori_loop(0, NZ, one, 0)

    def to_partner(ref, k, i):
        src = ref.at[i * NC + far_c]
        copy = remote(src, r_core.at[k, i], s_rc.at[k, i], r_rc.at[k, i], c_peer)
        return copy

    pre_low = own.at[1]

    def back_ff(i, carry):
        m = block_of(i)
        outer(bl_t, hid.at[m], g_d, m, 0, width)
        grad = nn(bl[...], square(w_d, m, 0, width)) * gder[m]
        pre_low[...] = grad.astype(BF16)
        gs[0, pl.ds(BIAS_ROW + m, 1), :] = col_sum(pre_low[...].astype(F32))
        outer(low_t, pre_low, g_i, m, 0, width)
        acc[...] += nt(pre_low[...], square(w_i, m, 0, width))

        @pl.when(i < NY)
        def _():
            to_partner(g_d, 0, i).start()
            to_partner(g_i, 1, i).start()

        return carry

    lax.fori_loop(0, GROUP, back_ff, 0)

    top_rows = pl.ds(0, BWD_ROWS)
    low_rows = pl.ds(BWD_ROWS, block - BWD_ROWS)

    def add_core(k, ref):
        for yy in range(NY):
            m = yy * NC + c
            to_partner(ref, k, yy).wait_recv()

            def one(zz, carry):
                ref[m, zz] = ref[m, zz] + r_core[k, yy, zz]
                return carry

            lax.fori_loop(0, NZ, one, 0)

    def reduce_first(k, ref):
        push(
            ref.at[over_y, :, :, top_rows], r_yf.at[k], s_red.at[k, 0], r_red.at[k, 0], y_peer
        )
        for yy in range(NY):
            push(
                ref.at[yy * NC + c, :, far_x, low_rows],
                r_xf.at[k, yy],
                s_red.at[k, 1 + yy],
                r_red.at[k, 1 + yy],
                x_peer,
            )

    def reduce_second(k, ref):
        arrived(r_yf.at[k], s_red.at[k, 0], r_red.at[k, 0])
        ref[mine, :, :, top_rows, :] = ref[mine, :, :, top_rows, :] + r_yf[k]
        push(
            ref.at[mine, :, far_x, top_rows], r_xs.at[k], s_red.at[k, 3], r_red.at[k, 3], x_peer
        )
        for yy in range(NY):
            m = yy * NC + c
            arrived(r_xf.at[k, yy], s_red.at[k, 1 + yy], r_red.at[k, 1 + yy])
            ref[m, :, x, low_rows, :] = ref[m, :, x, low_rows, :] + r_xf[k, yy]
        push(
            ref.at[over_y, :, x, low_rows], r_ys.at[k], s_red.at[k, 4], r_red.at[k, 4], y_peer
        )

    def reduce_third(k, ref):
        arrived(r_xs.at[k], s_red.at[k, 3], r_red.at[k, 3])
        ref[mine, :, x, top_rows, :] = ref[mine, :, x, top_rows, :] + r_xs[k]
        arrived(r_ys.at[k], s_red.at[k, 4], r_red.at[k, 4])
        ref[mine, :, x, low_rows, :] = ref[mine, :, x, low_rows, :] + r_ys[k]
        for step in range(1, NZ):
            push(
                ref.at[mine, z_at(step), x],
                r_z.at[k, step - 1],
                s_rz.at[k, step],
                r_rz.at[k, step],
                z_peer(step),
            )

    def reduce_last(k, ref, result):
        total = ref[mine, z, x].astype(F32)
        for step in range(1, NZ):
            arrived(r_z.at[k, step - 1], s_rz.at[k, step], r_rz.at[k, step])
            total = total + r_z[k, step - 1].astype(F32)
        result[...] = total

    add_core(0, g_d)
    reduce_first(0, g_d)
    add_core(1, g_i)
    reduce_first(1, g_i)
    forward_result(0)

    xhat = xh1[...]
    normed_grad = acc[...]
    gs[0, 0:1, :] = col_sum(normed_grad * xhat)
    gs[0, 3:4, :] = col_sum(normed_grad)
    first_grad = norm_back(normed_grad, xhat, rs1[...], par_row(0))
    gs[0, 2:3, :] = col_sum(first_grad)
    acc[...] = first_grad
    bl[...] = first_grad.astype(BF16)
    bl_t[...] = bl[...].T
    low_t[...] = xs[...].T
    finish(PILOT)
    reduce_second(0, g_d)

    g_a = w_d

    def back_attention(i, carry):
        m = block_of(i)
        outer(bl_t, ctx.at[m], g_a, m, qkv_cols, width)
        context_grad = nn(bl[...], square(w_a, m, qkv_cols, width)).astype(BF16)
        part = qkv[m]
        for h in range(heads_here):
            lo = h * HEAD_DIM
            q = part[:, lo : lo + HEAD_DIM]
            k = part[:, head_cols + lo : head_cols + lo + HEAD_DIM]
            v = part[:, 2 * head_cols + lo : 2 * head_cols + lo + HEAD_DIM]
            d_ctx = context_grad[:, lo : lo + HEAD_DIM]
            weight = prob[m * heads_here + h]
            d_value = tn(weight.astype(BF16), d_ctx)
            d_prob = nt(d_ctx, v)
            spread = jnp.sum(weight * d_prob, -1, keepdims=True)
            d_score = (weight * (d_prob - spread)).astype(BF16)
            qg[:, lo : lo + HEAD_DIM] = (nn(d_score, k) * scale).astype(BF16)
            qg[:, head_cols + lo : head_cols + lo + HEAD_DIM] = (tn(d_score, q) * scale).astype(BF16)
            qg[:, 2 * head_cols + lo : 2 * head_cols + lo + HEAD_DIM] = d_value.astype(BF16)
        gs[0, pl.ds(QKV_ROW + m, 1), :qkv_cols] = col_sum(qg[...].astype(F32))
        outer(low_t, qg, g_a, m, 0, qkv_cols)
        acc[...] += nt(qg[...], square(w_a, m, 0, qkv_cols))

        @pl.when(i < NY)
        def _():
            to_partner(g_a, 2, i).start()

        return carry

    for chunk, copy in sends:
        if chunk == DOWN:
            copy.wait_send()
    lax.fori_loop(0, GROUP, back_attention, 0)
    small_stage(1, gs, gs_in, 0)
    own[2] = acc[...].astype(BF16)
    send_result(2)
    small_add(1, gs, gs_in, 0)
    small_stage(1, gs, gs_in, 1)
    add_core(2, g_a)
    reduce_first(2, g_a)
    reduce_second(1, g_i)
    small_add(1, gs, gs_in, 1)
    small_stage(1, gs, gs_in, 2)

    acc[...] = jnp.zeros_like(acc)

    def steer(m, carry):
        acc[...] += nt(hid[m], square(w_p, m, 0, width))
        return carry

    lax.fori_loop(0, GROUP, steer, 0)
    tangent = acc[...]
    xhat = xh2[...]
    along = rs2[...] * (tangent - row_mean(tangent) - xhat * row_mean(tangent * xhat))
    own[1] = (par_row(1) * along).astype(BF16)
    send_result(1)
    small_add(1, gs, gs_in, 2)
    small_stage(1, gs, gs_in, 3)
    reduce_third(0, g_d)
    forward_result(2)
    reduce_third(1, g_i)
    reduce_second(2, g_a)
    forward_result(1)
    small_sum[...] = small_last(1, gs, gs_in)
    reduce_last(0, g_d, grad_d)
    reduce_last(1, g_i, grad_i)
    reduce_third(2, g_a)
    reduce_last(2, g_a, grad_a)
    for index in range(3):
        finish_result(index)
    for k, ref in enumerate((g_d, g_i, g_a)):
        for i in range(NY):
            to_partner(ref, k, i).wait_send()
    for chunk, copy in sends:
        if chunk != DOWN:
            copy.wait_send()


def run_layer(inner, lens, tok, cot, shards, small):
    width = tok.shape[1]
    rows = tok.shape[0] // GROUP
    block = width // BLOCKS
    head_cols = width // GROUP
    qkv_cols = 3 * head_cols
    heads = width // HEAD_DIM
    anywhere = pl.BlockSpec(memory_space=pl.ANY)
    vmem = pl.BlockSpec(memory_space=pltpu.VMEM)
    weight = pltpu.VMEM((GROUP, NZ, NX, block, width), BF16)
    act = pltpu.VMEM((rows, width), F32)
    act_low = pltpu.VMEM((rows, width), BF16)
    column = pltpu.VMEM((rows, 1), F32)
    dma = pltpu.SemaphoreType.DMA
    grads = 3
    scratch = (
        [weight] * 6
        + [
            pltpu.VMEM((grads, NY, NZ, NX, block, width), BF16),
            pltpu.VMEM((grads, NZ, NX, BWD_ROWS, width), BF16),
            pltpu.VMEM((grads, NY, NZ, block - BWD_ROWS, width), BF16),
            pltpu.VMEM((grads, NZ, BWD_ROWS, width), BF16),
            pltpu.VMEM((grads, NZ, block - BWD_ROWS, width), BF16),
            pltpu.VMEM((grads, NZ - 1, block, width), BF16),
            pltpu.VMEM((5, SMALL_ROWS, width), F32),
            pltpu.VMEM((6, SMALL_ROWS, width), F32),
            pltpu.VMEM((4, SMALL_ROWS, width), F32),
            pltpu.VMEM((6, SMALL_ROWS, width), F32),
            act_low,
            act_low,
            pltpu.VMEM((GROUP, rows, qkv_cols), BF16),
            pltpu.VMEM((heads, rows, rows), F32),
            pltpu.VMEM((GROUP, rows, head_cols), BF16),
            act,
            act,
            column,
            act_low,
            pltpu.VMEM((width, rows), BF16),
            pltpu.VMEM((GROUP, rows, width), BF16),
            pltpu.VMEM((GROUP, rows, width), F32),
            act,
            column,
            act,
            act_low,
            pltpu.VMEM((width, rows), BF16),
            pltpu.VMEM((rows, qkv_cols), BF16),
            pltpu.VMEM((3, rows, width), BF16),
        ]
        + [dma((7,))]
        + [dma((4, NZ))] * 12
        + [dma((grads, NY))] * 2
        + [dma((grads, 5))] * 2
        + [dma((grads, NZ))] * 2
        + [dma((2, 6))] * 2
        + [dma((3, 3))] * 2
        + [dma((3,))]
    )
    whole = jax.ShapeDtypeStruct(tok.shape, BF16)
    piece = jax.ShapeDtypeStruct((block, width), F32)
    return pl.pallas_call(
        functools.partial(layer_kernel, inner),
        out_shape=(
            whole,
            whole,
            whole,
            piece,
            piece,
            piece,
            jax.ShapeDtypeStruct((SMALL_ROWS, width), F32),
        ),
        in_specs=[pl.BlockSpec(memory_space=pltpu.SMEM)] + [anywhere] * 7,
        out_specs=(anywhere,) * 3 + (vmem,) * 4,
        scratch_shapes=scratch,
        compiler_params=pltpu.CompilerParams(
            collective_id=0, has_side_effects=True, vmem_limit_bytes=67043328
        ),
        name="layer",
    )(lens, tok, cot, *shards, small)


def local(
    tokens, cotangent, lengths, w_qkv, qv_bias, w_out, w_in, in_bias, w_down, pilot, gains, shifts
):
    n_dp = lax.axis_size("dp")
    inner = n_dp // BLOCKS
    groups = [[b * inner + i for i in range(inner)] for b in range(BLOCKS)]
    dp = lax.axis_index("dp")
    mp = lax.axis_index("mp")
    width = tokens.shape[1]
    head_cols = w_out.shape[0]
    local_rows = w_qkv.shape[0]
    shards = (
        jnp.concatenate([w_qkv.reshape(local_rows, 3 * head_cols), w_out.T], 1),
        w_in,
        w_down.T,
        pilot.T,
    )

    spot = jnp.arange(width, dtype=jnp.int32)
    share = gains.shape[1]

    def spread(values, period, offset):
        per = values.shape[1]
        tiled = jnp.tile(values, (1, period // per))
        tiled = jnp.pad(tiled, ((0, 0), (offset, width - offset - period)))
        place = (spot - offset) // per == dp
        return jnp.where(place & (spot >= offset) & (spot < offset + period), tiled, 0)

    head = (mp == 0).astype(F32)
    vectors = spread(jnp.concatenate([gains, shifts], 0).astype(F32), width, 0) * head
    at_mp = (jnp.arange(GROUP) == mp).astype(F32)[:, None]
    hidden_bias = spread(in_bias.astype(F32), width, 0) * at_mp
    pair = qv_bias.reshape(2, -1).astype(F32)
    qkv_bias = (
        spread(pair[0:1], head_cols, 0) + spread(pair[1:2], head_cols, 2 * head_cols)
    ) * at_mp
    small = jnp.concatenate(
        [
            vectors,
            hidden_bias,
            qkv_bias,
            jnp.zeros((SMALL_ROWS - QKV_ROW - GROUP, width), F32),
        ],
        0,
    )
    if inner > 1:
        shards = tuple(
            lax.all_gather(item, "dp", axis=0, tiled=True, axis_index_groups=groups)
            for item in shards
        )
        small = lax.psum(small, "dp", axis_index_groups=groups)

    out, along, input_grad, grad_a, grad_i, grad_d, sums = run_layer(
        inner, lengths, tokens, cotangent, shards, small
    )
    if inner > 1:
        grad_a, grad_i, grad_d = (
            lax.psum_scatter(
                item, "dp", scatter_dimension=0, tiled=True, axis_index_groups=groups
            )
            for item in (grad_a, grad_i, grad_d)
        )
        sums = lax.psum(sums, "dp", axis_index_groups=groups)

    columns = lax.dynamic_slice_in_dim(sums, dp * share, share, 1)
    bias_share = qv_bias.shape[2]
    bias_row = lax.dynamic_slice_in_dim(sums, QKV_ROW + mp, 1, 0)
    grad_qvb = jnp.stack(
        [
            lax.dynamic_slice_in_dim(bias_row, dp * bias_share, bias_share, 1),
            lax.dynamic_slice_in_dim(
                bias_row, 2 * head_cols + dp * bias_share, bias_share, 1
            ),
        ]
    )
    return (
        out,
        input_grad.astype(F32),
        along.astype(F32),
        grad_a[:, : 3 * head_cols].reshape(local_rows, 3, head_cols),
        grad_qvb,
        grad_a[:, 3 * head_cols :].T,
        grad_i,
        lax.dynamic_slice_in_dim(columns, BIAS_ROW + mp, 1, 0),
        grad_d.T,
        columns[0:2],
        columns[2:6],
    )


def solution(mesh):
    in_specs = (
        P("dp", None),
        P("dp", None),
        P("dp"),
        P("dp", None, "mp"),
        P(None, "mp", "dp"),
        P("mp", "dp"),
        P("dp", "mp"),
        P("mp", "dp"),
        P("mp", "dp"),
        P("mp", "dp"),
        P(None, "dp"),
        P(None, "dp"),
    )
    out_specs = (
        P("dp", None),
        P("dp", None),
        P("dp", None),
        P("dp", None, "mp"),
        P(None, "mp", "dp"),
        P("mp", "dp"),
        P("dp", "mp"),
        P("mp", "dp"),
        P("mp", "dp"),
        P(None, "dp"),
        P(None, "dp"),
    )
    return jax.shard_map(local, mesh=mesh, in_specs=in_specs, out_specs=out_specs, check_vma=False)
```

time: 942 us -> 242 us (0.26); the launches traced: 928 us -> 239 us
  waiting for transfers between devices: 453 us -> 0 us
  blocking collectives: 276 us -> 0 us
  Pallas kernels: 0 us -> 217 us
  matrix products: 63.8 us -> 0 us
  local copies, waits for them, and re-layouts: 68.1 us -> 11.7 us
  other arithmetic: 47.2 us -> 9.48 us
  between operations: 18.6 us -> 0.72 us
    reduce_scatter x13 -> x0, waiting for transfers between devices: 322 us -> none  [the longest x1 72.8 us: local(): lax.psum_scatter(totals[0], 'dp', scatter_dimension=0, tiled=True)]
    all_gather x19 -> x0, blocking collectives: 248 us -> none  [the longest x2 40.9 us: micro_step(): lax.all_gather(normed.astype(jnp.bfloat16), 'mp', axis=0, tiled=True)]
    pallas_call x0 -> x1, Pallas kernels: none -> 217 us  [run_layer(): pl.pallas_call(functools.partial(layer_kernel, inner), out_shape=(whole,...]
    unnamed x24 -> x0, waiting for transfers between devices: 114 us -> none
    dot_general x38 -> x0, matrix products: 63.8 us -> none  [the longest x2 14 us: micro_step(): jnp.dot(normed_low, full_in, preferred_element_type=jnp.float32)]
    unnamed x217 -> x17, local copies, waits for them, and re-layouts: 34.3 us -> 6.17 us
    unnamed x2 -> x0, blocking collectives: 27.6 us -> none
    reduce_sum x18 -> x0, other arithmetic: 18 us -> none  [the longest x4 6.09 us: affine_norm(): centered_input = stream - jnp.mean(stream, -1, keepdims=True)]
  transfers between devices with their start and end apart: 20 -> 0, of which waited for: 13 -> 0; matrix products, arithmetic and copies ran while one was open for 15% -> 0% of each run, Pallas kernels for 0% -> 0%
where the time goes in v1:
time: 242 us; the launch traced here: 239 us
  Pallas kernels  217 us (90%)
  local copies, waits for them, and re-layouts  11.7 us (5%)
  other arithmetic  9.48 us (4%)
    pallas_call x1, Pallas kernels, run_layer(): pl.pallas_call(functools.partial(layer_kernel, inner), out_shape=(whole,...  217 us
    unnamed x17, local copies, waits for them, and re-layouts  6.17 us

profile of v1, /device:TPU:25, one launch (start us, length us, event | category | flops | bytes accessed | tf_op | source)
XLA Modules:
  0.0 238.9 jit_solution(242114960782196579)
XLA Ops:
  0.6 0.9 copy.28
  1.5 1.1 copy.27
  2.6 0.2 copy.29
  2.8 0.8 pad_maximum_fusion.shard_a
  3.5 0.7 bitcast_convert_fusion
  4.2 0.1 tile.49
  4.3 0.7 convert_element_type.41
  4.9 0.1 tile.55
  5.0 0.1 tile.52
  5.1 0.1 broadcast_multiply_fusion.1
  5.2 0.7 maximum_convert_fusion
  5.9 0.1 tile.45
  6.0 0.1 pad.15.clone
  6.1 0.7 maximum_maximum_fusion.small
  6.8 216.9 %layer.1 = (bf16[1024,768]{1,0:T(8,128)(2,1)}, bf16[1024,768]{1,0:T(8,128)(2,1)}, bf16[1024,768]{1,0:T(8,128)(2,1)}, f32[96,768]{1,0:T(8,128)}, f32[96,768]{1,0:...) custom-call(s32[4]{0:T(128)} %lens.1, bf16[1024,768]{1,0:T(8,128)(2,1)} %tok.1, bf16[1024,768]{1,0:T(8,128)(2,1)} %cot.1, ...), custom_call_target="tpu_custom_call" | custom-call | tf_op jit(solution)/shard_map/layer/pallas_call | solution.py:714
  223.7 0.0 copy-start.1
  223.8 3.4 %convert_element_type.42 = f32[1024,768]{1,0:T(8,128)} convert(bf16[1024,768]{1,0:T(8,128)(2,1)} %get-tuple-element.19) | non-fusion elementwise | flops 786432 | bytes 4718592 | tf_op jit(solution)/shard_map/convert_element_type | solution.py:812
  227.2 0.0 copy-done.1
  227.2 0.0 copy-start.2
  227.2 1.9 convert_element_type.43
  229.1 0.0 copy-start
  229.1 0.0 copy-done.2
  229.1 0.1 copy.30
  229.3 0.9 copy.31
  230.1 0.8 dynamic-slice_bitcast_fusion.1
  230.9 0.6 pad_maximum_fusion.1
  231.5 0.1 slice_bitcast_fusion
  231.6 0.7 copy.32
  232.3 1.3 dynamic_slice.15
  233.6 1.3 constant_dynamic-slice_fusion
  234.9 1.3 dynamic-slice.1
  236.3 0.0 copy-done
  236.3 0.0 copy-start.4
  236.3 0.0 copy-start.3
  236.3 1.1 copy.36
  237.4 0.0 copy-done.4
  237.4 0.7 copy.37
  238.1 0.0 copy-done.3
  238.1 0.7 copy.38
  (12 shorter events, 0.1 us)
Async XLA Ops:
  223.7 3.4 %copy-start.1 = (bf16[1024,768]{1,0:T(8,128)(2,1)S(1)}, bf16[1024,768]{1,0:T(8,128)(2,1)}, u32[]{:S(2)}) copy-start(bf16[1024,768]{1,0:T(8,128)(2,1)} %get-tuple-element.20) | copy-start | bytes 4718596
  227.2 1.9 copy-start.2
  229.1 7.2 %copy-start = (bf16[1024,768]{1,0:T(8,128)(2,1)S(1)}, bf16[1024,768]{1,0:T(8,128)(2,1)}, u32[]{:S(2)}) copy-start(bf16[1024,768]{1,0:T(8,128)(2,1)} %get-tuple-element.64) | copy-start | bytes 4718596
  236.3 1.1 copy-start.4
  236.3 1.9 copy-start.3

commit v2 on v1

--- a/solution.py
+++ b/solution.py
@@ -304,14 +304,17 @@
         copy.wait()
     to_core(QKV, 0, mine, x)
     send_own(IN)
-    for step in range(NZ):
-        forward_diagonal(QKV, step)
+    forward_diagonal(QKV, 0)
+    forward_diagonal(QKV, 1)
+    forward_z(IN, 1)
+    forward_diagonal(QKV, 3)
+    forward_z(IN, 3)
+    forward_diagonal(QKV, 2)
     to_core(QKV, 1, mine, far_x)
     to_core(QKV, 2, over_y, x)
+    forward_z(IN, 2)
+    to_core(IN, 0, mine, x)
     par[4] = small_last(0, par, par_in)
-    for step in (1, 3, 2):
-        forward_z(IN, step)
-    to_core(IN, 0, mine, x)
     finish(QKV)
 
     length = lens[mp]
@@ -346,15 +349,28 @@
             ctx[m, :, lo : lo + HEAD_DIM] = nn(weight.astype(BF16), v).astype(BF16)
         return carry
 
-    for step in range(NZ):
-        forward_diagonal(IN, step)
-    to_core(IN, 1, mine, far_x)
-    to_core(IN, 2, over_y, x)
-    send_own(DOWN)
+    def next_chunk(k, part):
+        if part == 0:
+            if k < PILOT:
+                send_own(k + 1)
+            forward_diagonal(k, 0)
+            forward_diagonal(k, 1)
+            if k < PILOT:
+                forward_z(k + 1, 1)
+            return
+        forward_diagonal(k, 3)
+        if k < PILOT:
+            forward_z(k + 1, 3)
+        forward_diagonal(k, 2)
+        to_core(k, 1, mine, far_x)
+        to_core(k, 2, over_y, x)
+        if k < PILOT:
+            forward_z(k + 1, 2)
+            to_core(k + 1, 0, mine, x)
+
+    next_chunk(IN, 0)
     lax.fori_loop(0, GROUP, attend, 0)
-    for step in (1, 3, 2):
-        forward_z(DOWN, step)
-    to_core(DOWN, 0, mine, x)
+    next_chunk(IN, 1)
 
     acc[...] = jnp.zeros_like(acc)
 
@@ -372,11 +388,7 @@
     normed_low = (xhat * par_row(0) + par_row(3)).astype(BF16)
     low[...] = normed_low
     finish(IN)
-    for step in range(NZ):
-        forward_diagonal(DOWN, step)
-    to_core(DOWN, 1, mine, far_x)
-    to_core(DOWN, 2, over_y, x)
-    send_own(PILOT)
+    next_chunk(DOWN, 0)
 
     def expand(m, carry):
         pre = nn(low[...], square(w_i, m, 0, width)) + par[4, pl.ds(BIAS_ROW + m, 1), :]
@@ -387,9 +399,7 @@
 
     lax.fori_loop(0, GROUP, expand, 0)
     low_t[...] = low[...].T
-    for step in (1, 3, 2):
-        forward_z(PILOT, step)
-    to_core(PILOT, 0, mine, x)
+    next_chunk(DOWN, 1)
     finish(DOWN)
 
     acc[...] = xh1[...] * par_row(0) + par_row(3) + par_row(4)
@@ -399,10 +409,7 @@
         return carry
 
     lax.fori_loop(0, GROUP, contract, 0)
-    for step in range(NZ):
-        forward_diagonal(PILOT, step)
-    to_core(PILOT, 1, mine, far_x)
-    to_core(PILOT, 2, over_y, x)
+    next_chunk(PILOT, 0)
 
     stream = acc[...]
     centered = stream - row_mean(stream)
@@ -452,8 +459,7 @@
     acc[...] = stream_grad
 
     def block_of(i):
-        other = i < NY
-        return jnp.where(other, i * NC + far_c, (i - NY) * NC + c)
+        return i * NC + far_c if i < NY else (i - NY) * NC + c
 
     slab = NX * block
 
@@ -473,7 +479,7 @@
 
     pre_low = own.at[1]
 
-    def back_ff(i, carry):
+    def back_ff(i):
         m = block_of(i)
         outer(bl_t, hid.at[m], g_d, m, 0, width)
         grad = nn(bl[...], square(w_d, m, 0, width)) * gder[m]
@@ -482,14 +488,14 @@
         outer(low_t, pre_low, g_i, m, 0, width)
         acc[...] += nt(pre_low[...], square(w_i, m, 0, width))
 
-        @pl.when(i < NY)
-        def _():
+        if i < NY:
             to_partner(g_d, 0, i).start()
             to_partner(g_i, 1, i).start()
 
-        return carry
-
-    lax.fori_loop(0, GROUP, back_ff, 0)
+    for i in range(GROUP):
+        back_ff(i)
+        if i == 0:
+            next_chunk(PILOT, 1)
 
     top_rows = pl.ds(0, BWD_ROWS)
     low_rows = pl.ds(BWD_ROWS, block - BWD_ROWS)
@@ -569,12 +575,9 @@
     bl[...] = first_grad.astype(BF16)
     bl_t[...] = bl[...].T
     low_t[...] = xs[...].T
-    finish(PILOT)
-    reduce_second(0, g_d)
-
     g_a = w_d
 
-    def back_attention(i, carry):
+    def back_attention(i):
         m = block_of(i)
         outer(bl_t, ctx.at[m], g_a, m, qkv_cols, width)
         context_grad = nn(bl[...], square(w_a, m, qkv_cols, width)).astype(BF16)
@@ -597,26 +600,25 @@
         outer(low_t, qg, g_a, m, 0, qkv_cols)
         acc[...] += nt(qg[...], square(w_a, m, 0, qkv_cols))
 
-        @pl.when(i < NY)
-        def _():
+        if i < NY:
             to_partner(g_a, 2, i).start()
-
-        return carry
 
     for chunk, copy in sends:
         if chunk == DOWN:
             copy.wait_send()
-    lax.fori_loop(0, GROUP, back_attention, 0)
+    for i in range(GROUP):
+        back_attention(i)
+        if i == 2:
+            finish(PILOT)
+            reduce_second(0, g_d)
+    own[2] = acc[...].astype(BF16)
+    add_core(2, g_a)
+    reduce_first(2, g_a)
+    send_result(2)
     small_stage(1, gs, gs_in, 0)
-    own[2] = acc[...].astype(BF16)
-    send_result(2)
+    reduce_second(1, g_i)
     small_add(1, gs, gs_in, 0)
     small_stage(1, gs, gs_in, 1)
-    add_core(2, g_a)
-    reduce_first(2, g_a)
-    reduce_second(1, g_i)
-    small_add(1, gs, gs_in, 1)
-    small_stage(1, gs, gs_in, 2)
 
     acc[...] = jnp.zeros_like(acc)
 
@@ -630,17 +632,19 @@
     along = rs2[...] * (tangent - row_mean(tangent) - xhat * row_mean(tangent * xhat))
     own[1] = (par_row(1) * along).astype(BF16)
     send_result(1)
+    reduce_third(0, g_d)
+    small_add(1, gs, gs_in, 1)
+    small_stage(1, gs, gs_in, 2)
+    reduce_second(2, g_a)
+    reduce_third(1, g_i)
     small_add(1, gs, gs_in, 2)
     small_stage(1, gs, gs_in, 3)
-    reduce_third(0, g_d)
+    reduce_last(0, g_d, grad_d)
     forward_result(2)
-    reduce_third(1, g_i)
-    reduce_second(2, g_a)
+    reduce_third(2, g_a)
     forward_result(1)
+    reduce_last(1, g_i, grad_i)
     small_sum[...] = small_last(1, gs, gs_in)
-    reduce_last(0, g_d, grad_d)
-    reduce_last(1, g_i, grad_i)
-    reduce_third(2, g_a)
     reduce_last(2, g_a, grad_a)
     for index in range(3):
         finish_result(index)

time: 242 us -> 229 us (0.946); the launches traced: 239 us -> 229 us
  Pallas kernels: 217 us -> 207 us
    pallas_call x1, Pallas kernels: 217 us -> 207 us  [run_layer(): pl.pallas_call(functools.partial(layer_kernel, inner), out_shape=(whole,...]
where the time goes in v2:
time: 229 us
  Pallas kernels  207 us (90%)
  local copies, waits for them, and re-layouts  11.7 us (5%)
  other arithmetic  9.48 us (4%)
    pallas_call x1, Pallas kernels, run_layer(): pl.pallas_call(functools.partial(layer_kernel, inner), out_shape=(whole,...  207 us
    unnamed x17, local copies, waits for them, and re-layouts  6.17 us

profile of v2, /device:TPU:25, one launch (start us, length us, event | category | flops | bytes accessed | tf_op | source)
XLA Modules:
  0.0 228.6 jit_solution(4217832620828702759)
XLA Ops:
  0.6 0.9 copy.28
  1.5 1.1 copy.27
  2.6 0.2 copy.29
  2.8 0.8 pad_maximum_fusion.shard_a
  3.5 0.7 bitcast_convert_fusion
  4.2 0.1 tile.49
  4.3 0.7 convert_element_type.41
  4.9 0.1 tile.55
  5.0 0.1 tile.52
  5.1 0.1 broadcast_multiply_fusion.1
  5.2 0.7 maximum_convert_fusion
  5.9 0.1 tile.45
  6.0 0.1 pad.15.clone
  6.1 0.7 maximum_maximum_fusion.small
  6.8 206.7 %layer.1 = (bf16[1024,768]{1,0:T(8,128)(2,1)}, bf16[1024,768]{1,0:T(8,128)(2,1)}, bf16[1024,768]{1,0:T(8,128)(2,1)}, f32[96,768]{1,0:T(8,128)}, f32[96,768]{1,0:...) custom-call(s32[4]{0:T(128)} %lens.1, bf16[1024,768]{1,0:T(8,128)(2,1)} %tok.1, bf16[1024,768]{1,0:T(8,128)(2,1)} %cot.1, ...), custom_call_target="tpu_custom_call" | custom-call | tf_op jit(solution)/shard_map/layer/pallas_call | solution.py:718
  213.5 0.0 copy-start.1
  213.5 3.4 %convert_element_type.42 = f32[1024,768]{1,0:T(8,128)} convert(bf16[1024,768]{1,0:T(8,128)(2,1)} %get-tuple-element.19) | non-fusion elementwise | flops 786432 | bytes 4718592 | tf_op jit(solution)/shard_map/convert_element_type | solution.py:816
  216.9 0.0 copy-done.1
  216.9 0.0 copy-start.2
  216.9 1.9 convert_element_type.43
  218.8 0.0 copy-start
  218.8 0.0 copy-done.2
  218.8 0.1 copy.30
  219.0 0.9 copy.31
  219.9 0.8 dynamic-slice_bitcast_fusion.1
  220.7 0.6 pad_maximum_fusion.1
  221.2 0.1 slice_bitcast_fusion
  221.3 0.7 copy.32
  222.1 1.3 dynamic_slice.15
  223.3 1.3 constant_dynamic-slice_fusion
  224.7 1.3 dynamic-slice.1
  226.0 0.0 copy-done
  226.0 0.0 copy-start.4
  226.0 0.0 copy-start.3
  226.0 1.1 copy.36
  227.2 0.0 copy-done.4
  227.2 0.7 copy.37
  227.9 0.0 copy-done.3
  227.9 0.7 copy.38
  (12 shorter events, 0.1 us)
Async XLA Ops:
  213.5 3.4 %copy-start.1 = (bf16[1024,768]{1,0:T(8,128)(2,1)S(1)}, bf16[1024,768]{1,0:T(8,128)(2,1)}, u32[]{:S(2)}) copy-start(bf16[1024,768]{1,0:T(8,128)(2,1)} %get-tuple-element.20) | copy-start | bytes 4718596
  216.9 1.9 copy-start.2
  218.8 7.2 %copy-start = (bf16[1024,768]{1,0:T(8,128)(2,1)S(1)}, bf16[1024,768]{1,0:T(8,128)(2,1)}, u32[]{:S(2)}) copy-start(bf16[1024,768]{1,0:T(8,128)(2,1)} %get-tuple-element.64) | copy-start | bytes 4718596
  226.0 1.1 copy-start.4
  226.0 1.9 copy-start.3

commit v3 on v2

--- a/solution.py
+++ b/solution.py
@@ -226,6 +226,10 @@
         src = weights[k].at[block_index, :, column]
         push(src, src, s_c.at[k, index], r_c.at[k, index], c_peer, k)
 
+    def columns_to_core(k):
+        to_core(k, 1, mine, far_x)
+        to_core(k, 2, over_y, x)
+
     def finish(k):
         for step in range(NZ):
             arrived(
@@ -288,30 +292,31 @@
     send_own(QKV)
     load_small.wait()
     small_stage(0, par, par_in, 0)
+    send_own(IN)
     send_z(IN)
     small_add(0, par, par_in, 0)
     small_stage(0, par, par_in, 1)
     forward_z(QKV, 1)
     small_add(0, par, par_in, 1)
     small_stage(0, par, par_in, 2)
+    forward_diagonal(QKV, 0)
     forward_z(QKV, 3)
     small_add(0, par, par_in, 2)
     small_stage(0, par, par_in, 3)
+    forward_diagonal(QKV, 1)
     forward_z(QKV, 2)
     send_z(DOWN)
     send_z(PILOT)
     for copy in loads:
         copy.wait()
     to_core(QKV, 0, mine, x)
-    send_own(IN)
-    forward_diagonal(QKV, 0)
-    forward_diagonal(QKV, 1)
+    send_own(DOWN)
+    forward_diagonal(QKV, 3)
     forward_z(IN, 1)
-    forward_diagonal(QKV, 3)
+    forward_diagonal(QKV, 2)
+    columns_to_core(QKV)
     forward_z(IN, 3)
-    forward_diagonal(QKV, 2)
-    to_core(QKV, 1, mine, far_x)
-    to_core(QKV, 2, over_y, x)
+    forward_diagonal(IN, 0)
     forward_z(IN, 2)
     to_core(IN, 0, mine, x)
     par[4] = small_last(0, par, par_in)
@@ -349,28 +354,16 @@
             ctx[m, :, lo : lo + HEAD_DIM] = nn(weight.astype(BF16), v).astype(BF16)
         return carry
 
-    def next_chunk(k, part):
-        if part == 0:
-            if k < PILOT:
-                send_own(k + 1)
-            forward_diagonal(k, 0)
-            forward_diagonal(k, 1)
-            if k < PILOT:
-                forward_z(k + 1, 1)
-            return
-        forward_diagonal(k, 3)
-        if k < PILOT:
-            forward_z(k + 1, 3)
-        forward_diagonal(k, 2)
-        to_core(k, 1, mine, far_x)
-        to_core(k, 2, over_y, x)
-        if k < PILOT:
-            forward_z(k + 1, 2)
-            to_core(k + 1, 0, mine, x)
-
-    next_chunk(IN, 0)
-    lax.fori_loop(0, GROUP, attend, 0)
-    next_chunk(IN, 1)
+    forward_diagonal(IN, 1)
+    send_own(PILOT)
+    forward_diagonal(IN, 3)
+    forward_z(DOWN, 1)
+    lax.fori_loop(0, NY, attend, 0)
+    forward_diagonal(IN, 2)
+    columns_to_core(IN)
+    forward_z(DOWN, 3)
+    forward_diagonal(DOWN, 0)
+    lax.fori_loop(NY, GROUP, attend, 0)
 
     acc[...] = jnp.zeros_like(acc)
 
@@ -387,8 +380,12 @@
     xh1[...] = xhat
     normed_low = (xhat * par_row(0) + par_row(3)).astype(BF16)
     low[...] = normed_low
+    forward_z(DOWN, 2)
+    to_core(DOWN, 0, mine, x)
+    forward_diagonal(DOWN, 1)
     finish(IN)
-    next_chunk(DOWN, 0)
+    forward_diagonal(DOWN, 3)
+    forward_z(PILOT, 1)
 
     def expand(m, carry):
         pre = nn(low[...], square(w_i, m, 0, width)) + par[4, pl.ds(BIAS_ROW + m, 1), :]
@@ -399,8 +396,14 @@
 
     lax.fori_loop(0, GROUP, expand, 0)
     low_t[...] = low[...].T
-    next_chunk(DOWN, 1)
+    forward_diagonal(DOWN, 2)
+    columns_to_core(DOWN)
+    forward_z(PILOT, 3)
+    forward_diagonal(PILOT, 0)
+    forward_z(PILOT, 2)
+    to_core(PILOT, 0, mine, x)
     finish(DOWN)
+    forward_diagonal(PILOT, 1)
 
     acc[...] = xh1[...] * par_row(0) + par_row(3) + par_row(4)
 
@@ -409,8 +412,6 @@
         return carry
 
     lax.fori_loop(0, GROUP, contract, 0)
-    next_chunk(PILOT, 0)
-
     stream = acc[...]
     centered = stream - row_mean(stream)
     rstd = lax.rsqrt(row_mean(centered * centered) + EPSILON)
@@ -440,6 +441,7 @@
         arrived(far, s_out.at[index, 2], r_out.at[index, 2])
 
     send_result(0)
+    forward_diagonal(PILOT, 3)
 
     gs[0] = jnp.zeros(gs.shape[1:], F32)
 
@@ -495,7 +497,8 @@
     for i in range(GROUP):
         back_ff(i)
         if i == 0:
-            next_chunk(PILOT, 1)
+            forward_diagonal(PILOT, 2)
+            columns_to_core(PILOT)
 
     top_rows = pl.ds(0, BWD_ROWS)
     low_rows = pl.ds(BWD_ROWS, block - BWD_ROWS)
@@ -613,10 +616,11 @@
             reduce_second(0, g_d)
     own[2] = acc[...].astype(BF16)
     add_core(2, g_a)
+    reduce_second(1, g_i)
     reduce_first(2, g_a)
     send_result(2)
     small_stage(1, gs, gs_in, 0)
-    reduce_second(1, g_i)
+    reduce_third(0, g_d)
     small_add(1, gs, gs_in, 0)
     small_stage(1, gs, gs_in, 1)
 
@@ -632,15 +636,14 @@
     along = rs2[...] * (tangent - row_mean(tangent) - xhat * row_mean(tangent * xhat))
     own[1] = (par_row(1) * along).astype(BF16)
     send_result(1)
-    reduce_third(0, g_d)
+    reduce_third(1, g_i)
     small_add(1, gs, gs_in, 1)
     small_stage(1, gs, gs_in, 2)
     reduce_second(2, g_a)
-    reduce_third(1, g_i)
+    reduce_last(0, g_d, grad_d)
+    forward_result(2)
     small_add(1, gs, gs_in, 2)
     small_stage(1, gs, gs_in, 3)
-    reduce_last(0, g_d, grad_d)
-    forward_result(2)
     reduce_third(2, g_a)
     forward_result(1)
     reduce_last(1, g_i, grad_i)

time: 229 us -> 217 us (0.948)
  Pallas kernels: 207 us -> 193 us
    pallas_call x1, Pallas kernels: 207 us -> 193 us  [run_layer(): pl.pallas_call(functools.partial(layer_kernel, inner), out_shape=(whole,...]
where the time goes in v3:
time: 217 us; the launch traced here: 215 us
  Pallas kernels  193 us (89%)
  local copies, waits for them, and re-layouts  11.7 us (5%)
  other arithmetic  9.48 us (4%)
    pallas_call x1, Pallas kernels, run_layer(): pl.pallas_call(functools.partial(layer_kernel, inner), out_shape=(whole,...  193 us
    unnamed x17, local copies, waits for them, and re-layouts  6.17 us

profile of v3, /device:TPU:25, one launch (start us, length us, event | category | flops | bytes accessed | tf_op | source)
XLA Modules:
  0.0 215.1 jit_solution(18037943066054772461)
XLA Ops:
  0.6 0.9 copy.28
  1.5 1.1 copy.27
  2.6 0.2 copy.29
  2.8 0.8 pad_maximum_fusion.shard_a
  3.5 0.7 bitcast_convert_fusion
  4.2 0.1 tile.49
  4.3 0.7 convert_element_type.41
  4.9 0.1 tile.55
  5.0 0.1 tile.52
  5.1 0.1 broadcast_multiply_fusion.1
  5.2 0.7 maximum_convert_fusion
  5.9 0.1 tile.45
  6.0 0.1 pad.15.clone
  6.1 0.7 maximum_maximum_fusion.small
  6.8 193.2 %layer.1 = (bf16[1024,768]{1,0:T(8,128)(2,1)}, bf16[1024,768]{1,0:T(8,128)(2,1)}, bf16[1024,768]{1,0:T(8,128)(2,1)}, f32[96,768]{1,0:T(8,128)}, f32[96,768]{1,0:...) custom-call(s32[4]{0:T(128)} %lens.1, bf16[1024,768]{1,0:T(8,128)(2,1)} %tok.1, bf16[1024,768]{1,0:T(8,128)(2,1)} %cot.1, ...), custom_call_target="tpu_custom_call" | custom-call | tf_op jit(solution)/shard_map/layer/pallas_call | solution.py:721
  200.0 0.0 copy-start.1
  200.0 3.4 %convert_element_type.42 = f32[1024,768]{1,0:T(8,128)} convert(bf16[1024,768]{1,0:T(8,128)(2,1)} %get-tuple-element.19) | non-fusion elementwise | flops 786432 | bytes 4718592 | tf_op jit(solution)/shard_map/convert_element_type | solution.py:819
  203.4 0.0 copy-done.1
  203.4 0.0 copy-start.2
  203.4 1.9 convert_element_type.43
  205.3 0.0 copy-start
  205.3 0.0 copy-done.2
  205.3 0.1 copy.30
  205.5 0.9 copy.31
  206.4 0.8 dynamic-slice_bitcast_fusion.1
  207.2 0.6 pad_maximum_fusion.1
  207.7 0.1 slice_bitcast_fusion
  207.8 0.7 copy.32
  208.6 1.3 dynamic_slice.15
  209.8 1.3 constant_dynamic-slice_fusion
  211.2 1.3 dynamic-slice.1
  212.5 0.0 copy-done
  212.5 0.0 copy-start.4
  212.5 0.0 copy-start.3
  212.5 1.1 copy.36
  213.7 0.0 copy-done.4
  213.7 0.7 copy.37
  214.4 0.0 copy-done.3
  214.4 0.7 copy.38
  (12 shorter events, 0.1 us)
Async XLA Ops:
  200.0 3.4 %copy-start.1 = (bf16[1024,768]{1,0:T(8,128)(2,1)S(1)}, bf16[1024,768]{1,0:T(8,128)(2,1)}, u32[]{:S(2)}) copy-start(bf16[1024,768]{1,0:T(8,128)(2,1)} %get-tuple-element.20) | copy-start | bytes 4718596
  203.4 1.9 copy-start.2
  205.3 7.2 %copy-start = (bf16[1024,768]{1,0:T(8,128)(2,1)S(1)}, bf16[1024,768]{1,0:T(8,128)(2,1)}, u32[]{:S(2)}) copy-start(bf16[1024,768]{1,0:T(8,128)(2,1)} %get-tuple-element.64) | copy-start | bytes 4718596
  212.5 1.1 copy-start.4
  212.5 1.9 copy-start.3

commit v4 on v3

--- a/solution.py
+++ b/solution.py
@@ -226,6 +226,31 @@
         src = weights[k].at[block_index, :, column]
         push(src, src, s_c.at[k, index], r_c.at[k, index], c_peer, k)
 
+    def side_z(k):
+        for step in range(1, NZ):
+            src = weights[k].at[mine, z, far_x]
+            push(src, src, s_x.at[k, step], r_x.at[k, step], z_peer(step), k)
+            src = weights[k].at[over_y, z, x]
+            push(src, src, s_y.at[k, step], r_y.at[k, step], z_peer(step), k)
+
+    def corner_z(k):
+        arrived(weights[k].at[over_y, z, far_x, first], s_dy.at[k, 0], r_dy.at[k, 0])
+        arrived(weights[k].at[over_y, z, far_x, second], s_dx.at[k, 0], r_dx.at[k, 0])
+        src = weights[k].at[over_y, z, far_x]
+        for step in range(1, NZ):
+            push(src, src, s_dx.at[k, step], r_dx.at[k, step], z_peer(step), k)
+
+    def finish_z(k):
+        for step in range(1, NZ):
+            at = z_from(step)
+            arrived(weights[k].at[mine, at, x], s_z.at[k, step], r_zs.at[k, step])
+            arrived(weights[k].at[mine, at, far_x], s_x.at[k, step], r_x.at[k, step])
+            arrived(weights[k].at[over_y, at, x], s_y.at[k, step], r_y.at[k, step])
+            arrived(weights[k].at[over_y, at, far_x], s_dx.at[k, step], r_dx.at[k, step])
+        to_core(k, 0, mine, x)
+        columns_to_core(k)
+        exchange_core(k)
+
     def columns_to_core(k):
         to_core(k, 1, mine, far_x)
         to_core(k, 2, over_y, x)
@@ -242,6 +267,9 @@
                 s_dx.at[k, step],
                 r_dx.at[k, step],
             )
+        exchange_core(k)
+
+    def exchange_core(k):
         to_core(k, 3, over_y, far_x)
         for index, (block_index, column) in enumerate(
             (
@@ -293,24 +321,23 @@
     load_small.wait()
     small_stage(0, par, par_in, 0)
     send_own(IN)
-    send_z(IN)
     small_add(0, par, par_in, 0)
     small_stage(0, par, par_in, 1)
+    send_own(DOWN)
     forward_z(QKV, 1)
     small_add(0, par, par_in, 1)
     small_stage(0, par, par_in, 2)
+    send_own(PILOT)
     forward_diagonal(QKV, 0)
     forward_z(QKV, 3)
     small_add(0, par, par_in, 2)
     small_stage(0, par, par_in, 3)
     forward_diagonal(QKV, 1)
     forward_z(QKV, 2)
-    send_z(DOWN)
-    send_z(PILOT)
+    send_z(IN)
     for copy in loads:
         copy.wait()
     to_core(QKV, 0, mine, x)
-    send_own(DOWN)
     forward_diagonal(QKV, 3)
     forward_z(IN, 1)
     forward_diagonal(QKV, 2)
@@ -319,6 +346,7 @@
     forward_diagonal(IN, 0)
     forward_z(IN, 2)
     to_core(IN, 0, mine, x)
+    send_z(DOWN)
     par[4] = small_last(0, par, par_in)
     finish(QKV)
 
@@ -355,13 +383,15 @@
         return carry
 
     forward_diagonal(IN, 1)
-    send_own(PILOT)
     forward_diagonal(IN, 3)
     forward_z(DOWN, 1)
+    forward_diagonal(PILOT, 0)
     lax.fori_loop(0, NY, attend, 0)
     forward_diagonal(IN, 2)
     columns_to_core(IN)
     forward_z(DOWN, 3)
+    send_z(PILOT)
+    side_z(PILOT)
     forward_diagonal(DOWN, 0)
     lax.fori_loop(NY, GROUP, attend, 0)
 
@@ -385,7 +415,7 @@
     forward_diagonal(DOWN, 1)
     finish(IN)
     forward_diagonal(DOWN, 3)
-    forward_z(PILOT, 1)
+    corner_z(PILOT)
 
     def expand(m, carry):
         pre = nn(low[...], square(w_i, m, 0, width)) + par[4, pl.ds(BIAS_ROW + m, 1), :]
@@ -398,12 +428,7 @@
     low_t[...] = low[...].T
     forward_diagonal(DOWN, 2)
     columns_to_core(DOWN)
-    forward_z(PILOT, 3)
-    forward_diagonal(PILOT, 0)
-    forward_z(PILOT, 2)
-    to_core(PILOT, 0, mine, x)
     finish(DOWN)
-    forward_diagonal(PILOT, 1)
 
     acc[...] = xh1[...] * par_row(0) + par_row(3) + par_row(4)
 
@@ -441,7 +466,6 @@
         arrived(far, s_out.at[index, 2], r_out.at[index, 2])
 
     send_result(0)
-    forward_diagonal(PILOT, 3)
 
     gs[0] = jnp.zeros(gs.shape[1:], F32)
 
@@ -483,7 +507,6 @@
 
     def back_ff(i):
         m = block_of(i)
-        outer(bl_t, hid.at[m], g_d, m, 0, width)
         grad = nn(bl[...], square(w_d, m, 0, width)) * gder[m]
         pre_low[...] = grad.astype(BF16)
         gs[0, pl.ds(BIAS_ROW + m, 1), :] = col_sum(pre_low[...].astype(F32))
@@ -491,14 +514,8 @@
         acc[...] += nt(pre_low[...], square(w_i, m, 0, width))
 
         if i < NY:
-            to_partner(g_d, 0, i).start()
             to_partner(g_i, 1, i).start()
 
-    for i in range(GROUP):
-        back_ff(i)
-        if i == 0:
-            forward_diagonal(PILOT, 2)
-            columns_to_core(PILOT)
 
     top_rows = pl.ds(0, BWD_ROWS)
     low_rows = pl.ds(BWD_ROWS, block - BWD_ROWS)
@@ -562,8 +579,14 @@
             total = total + r_z[k, step - 1].astype(F32)
         result[...] = total
 
+    for i in range(GROUP):
+        outer(bl_t, hid.at[block_of(i)], g_d, block_of(i), 0, width)
+        if i < NY:
+            to_partner(g_d, 0, i).start()
     add_core(0, g_d)
     reduce_first(0, g_d)
+    for i in range(GROUP):
+        back_ff(i)
     add_core(1, g_i)
     reduce_first(1, g_i)
     forward_result(0)
@@ -612,18 +635,16 @@
     for i in range(GROUP):
         back_attention(i)
         if i == 2:
-            finish(PILOT)
             reduce_second(0, g_d)
     own[2] = acc[...].astype(BF16)
+    small_stage(1, gs, gs_in, 0)
     add_core(2, g_a)
     reduce_second(1, g_i)
     reduce_first(2, g_a)
-    send_result(2)
-    small_stage(1, gs, gs_in, 0)
-    reduce_third(0, g_d)
     small_add(1, gs, gs_in, 0)
     small_stage(1, gs, gs_in, 1)
-
+    reduce_third(0, g_d)
+    finish_z(PILOT)
     acc[...] = jnp.zeros_like(acc)
 
     def steer(m, carry):
@@ -635,18 +656,19 @@
     xhat = xh2[...]
     along = rs2[...] * (tangent - row_mean(tangent) - xhat * row_mean(tangent * xhat))
     own[1] = (par_row(1) * along).astype(BF16)
-    send_result(1)
     reduce_third(1, g_i)
+    reduce_second(2, g_a)
     small_add(1, gs, gs_in, 1)
     small_stage(1, gs, gs_in, 2)
-    reduce_second(2, g_a)
+    send_result(2)
+    send_result(1)
     reduce_last(0, g_d, grad_d)
-    forward_result(2)
     small_add(1, gs, gs_in, 2)
     small_stage(1, gs, gs_in, 3)
     reduce_third(2, g_a)
+    reduce_last(1, g_i, grad_i)
+    forward_result(2)
     forward_result(1)
-    reduce_last(1, g_i, grad_i)
     small_sum[...] = small_last(1, gs, gs_in)
     reduce_last(2, g_a, grad_a)
     for index in range(3):

time: 217 us -> 189 us (0.87)
  Pallas kernels: 193 us -> 166 us
    pallas_call x1, Pallas kernels: 193 us -> 166 us  [run_layer(): pl.pallas_call(functools.partial(layer_kernel, inner), out_shape=(whole,...]
where the time goes in v4:
time: 189 us; the launch traced here: 188 us
  Pallas kernels  166 us (88%)
  local copies, waits for them, and re-layouts  11.7 us (6%)
  other arithmetic  9.48 us (5%)
    pallas_call x1, Pallas kernels, run_layer(): pl.pallas_call(functools.partial(layer_kernel, inner), out_shape=(whole,...  166 us
    unnamed x17, local copies, waits for them, and re-layouts  6.17 us

profile of v4, /device:TPU:25, one launch (start us, length us, event | category | flops | bytes accessed | tf_op | source)
XLA Modules:
  0.0 187.8 jit_solution(16496230470855339807)
XLA Ops:
  0.6 0.9 copy.28
  1.5 1.1 copy.27
  2.6 0.2 copy.29
  2.8 0.8 pad_maximum_fusion.shard_a
  3.5 0.7 bitcast_convert_fusion
  4.2 0.1 tile.49
  4.3 0.7 convert_element_type.41
  4.9 0.1 tile.55
  5.0 0.1 tile.52
  5.1 0.1 broadcast_multiply_fusion.1
  5.2 0.7 maximum_convert_fusion
  5.9 0.1 tile.45
  6.0 0.1 pad.15.clone
  6.1 0.7 maximum_maximum_fusion.small
  6.8 165.8 %layer.1 = (bf16[1024,768]{1,0:T(8,128)(2,1)}, bf16[1024,768]{1,0:T(8,128)(2,1)}, bf16[1024,768]{1,0:T(8,128)(2,1)}, f32[96,768]{1,0:T(8,128)}, f32[96,768]{1,0:...) custom-call(s32[4]{0:T(128)} %lens.1, bf16[1024,768]{1,0:T(8,128)(2,1)} %tok.1, bf16[1024,768]{1,0:T(8,128)(2,1)} %cot.1, ...), custom_call_target="tpu_custom_call" | custom-call | tf_op jit(solution)/shard_map/layer/pallas_call | solution.py:743
  172.7 0.0 copy-start.1
  172.7 3.4 %convert_element_type.42 = f32[1024,768]{1,0:T(8,128)} convert(bf16[1024,768]{1,0:T(8,128)(2,1)} %get-tuple-element.19) | non-fusion elementwise | flops 786432 | bytes 4718592 | tf_op jit(solution)/shard_map/convert_element_type | solution.py:841
  176.1 0.0 copy-done.1
  176.1 0.0 copy-start.2
  176.1 1.9 %convert_element_type.43 = f32[1024,768]{1,0:T(8,128)} convert(bf16[1024,768]{1,0:T(8,128)(2,1)S(1)} %copy-done.1) | non-fusion elementwise | flops 786432 | bytes 4718592 | tf_op jit(solution)/shard_map/convert_element_type | solution.py:842
  178.0 0.0 copy-start
  178.0 0.0 copy-done.2
  178.0 0.1 copy.30
  178.2 0.9 copy.31
  179.0 0.8 dynamic-slice_bitcast_fusion.1
  179.8 0.6 pad_maximum_fusion.1
  180.4 0.1 slice_bitcast_fusion
  180.5 0.7 copy.32
  181.2 1.3 dynamic_slice.15
  182.5 1.3 constant_dynamic-slice_fusion
  183.9 1.3 dynamic-slice.1
  185.2 0.0 copy-done
  185.2 0.0 copy-start.4
  185.2 0.0 copy-start.3
  185.2 1.1 copy.36
  186.3 0.0 copy-done.4
  186.3 0.7 copy.37
  187.1 0.0 copy-done.3
  187.1 0.7 copy.38
  (12 shorter events, 0.1 us)
Async XLA Ops:
  172.7 3.4 %copy-start.1 = (bf16[1024,768]{1,0:T(8,128)(2,1)S(1)}, bf16[1024,768]{1,0:T(8,128)(2,1)}, u32[]{:S(2)}) copy-start(bf16[1024,768]{1,0:T(8,128)(2,1)} %get-tuple-element.20) | copy-start | bytes 4718596
  176.1 1.9 %copy-start.2 = (f32[96,768]{1,0:T(8,128)S(1)}, f32[96,768]{1,0:T(8,128)}, u32[]{:S(2)}) copy-start(f32[96,768]{1,0:T(8,128)} %get-tuple-element.21) | copy-start | bytes 884740
  178.0 7.2 %copy-start = (bf16[1024,768]{1,0:T(8,128)(2,1)S(1)}, bf16[1024,768]{1,0:T(8,128)(2,1)}, u32[]{:S(2)}) copy-start(bf16[1024,768]{1,0:T(8,128)(2,1)} %get-tuple-element.64) | copy-start | bytes 4718596
  185.2 1.1 copy-start.4
  185.2 1.9 copy-start.3

commit v5 on v4

--- a/solution.py
+++ b/solution.py
@@ -36,6 +36,12 @@
     return jnp.dot(a, b, preferred_element_type=F32)
 
 
+def one_hot(rows, columns, offset, dtype=BF16):
+    row = lax.broadcasted_iota(jnp.int32, (rows, columns), 0)
+    column = lax.broadcasted_iota(jnp.int32, (rows, columns), 1)
+    return (row + offset == column).astype(F32).astype(dtype)
+
+
 def row_mean(v):
     return jnp.mean(v, -1, keepdims=True)
 
@@ -49,11 +55,15 @@
     lens,
     tok,
     cot,
-    shard_a,
     shard_i,
     shard_d,
     shard_p,
-    small,
+    w_qkv,
+    w_out,
+    gains,
+    shifts,
+    in_bias,
+    qv_bias,
     out_o,
     along_o,
     ig_o,
@@ -122,7 +132,6 @@
     s_own,
 ):
     weights = (w_a, w_i, w_d, w_p)
-    shards = (shard_a, shard_i, shard_d, shard_p)
     width = xs.shape[1]
     block = w_a.shape[3]
     head_cols = ctx.shape[2]
@@ -139,6 +148,7 @@
     y, c = mp // NC, mp % NC
     far_y, far_x, far_c = 1 - y, 1 - x, 1 - c
     mine = mp
+    shards = (w_a.at[mine, z, x], shard_i, shard_d, shard_p)
     over_y = far_y * NC + c
     x_peer = {"dp": (z * NX + far_x) * inner + rest, "mp": mp}
     y_peer = {"dp": dp, "mp": over_y}
@@ -177,10 +187,26 @@
     peers = [x_peer, y_peer, c_peer] + [z_peer(step) for step in range(1, NZ)]
     for peer in peers:
         pl.semaphore_signal(barrier, inc=1, device_id=peer, device_id_type=pl.DeviceIdType.MESH)
+
+    for part in range(3):
+        w_a[mine, z, x, :, part * head_cols : (part + 1) * head_cols] = w_qkv[part]
+    w_a[mine, z, x, :, qkv_cols:] = nt(one_hot(block, block, 0), w_out[...]).astype(BF16)
+    share = gains.shape[1]
+    bias_share = qv_bias.shape[1]
+    par[0] = jnp.zeros(par.shape[1:], F32)
+    everyone = one_hot(share, width, spot * share)
+    first_only = one_hot(share, width, jnp.where(mp == 0, spot * share, -width))
+    par[0, 0:2, :] = nn(gains[...], first_only)
+    par[0, 2:6, :] = nn(shifts[...], first_only)
+    par[0, pl.ds(BIAS_ROW + mp, 1), :] = nn(in_bias[...], everyone)
+    par[0, pl.ds(QKV_ROW + mp, 1), :] = nn(
+        qv_bias[0:1, :], one_hot(bias_share, width, spot * bias_share)
+    ) + nn(qv_bias[1:2, :], one_hot(bias_share, width, 2 * head_cols + spot * bias_share))
+
     pl.semaphore_wait(barrier, len(peers))
 
     loads = []
-    for k in range(4):
+    for k in range(1, 4):
         loads.append(
             pltpu.make_async_copy(shards[k], weights[k].at[mine, z, x], s_load.at[k])
         )
@@ -312,13 +338,10 @@
             total = total + term
         return total
 
-    load_small = pltpu.make_async_copy(small, par.at[0], s_load.at[6])
-    load_small.start()
     send_z(QKV)
     for copy in loads:
         copy.start()
     send_own(QKV)
-    load_small.wait()
     small_stage(0, par, par_in, 0)
     send_own(IN)
     small_add(0, par, par_in, 0)
@@ -681,7 +704,7 @@
             copy.wait_send()
 
 
-def run_layer(inner, lens, tok, cot, shards, small):
+def run_layer(inner, lens, tok, cot, shards, projections, small):
     width = tok.shape[1]
     rows = tok.shape[0] // GROUP
     block = width // BLOCKS
@@ -751,14 +774,114 @@
             piece,
             jax.ShapeDtypeStruct((SMALL_ROWS, width), F32),
         ),
-        in_specs=[pl.BlockSpec(memory_space=pltpu.SMEM)] + [anywhere] * 7,
+        in_specs=[pl.BlockSpec(memory_space=pltpu.SMEM)] + [anywhere] * 5 + [vmem] * 6,
         out_specs=(anywhere,) * 3 + (vmem,) * 4,
         scratch_shapes=scratch,
         compiler_params=pltpu.CompilerParams(
             collective_id=0, has_side_effects=True, vmem_limit_bytes=67043328
         ),
         name="layer",
-    )(lens, tok, cot, *shards, small)
+    )(lens, tok, cot, *shards, *projections, *small)
+
+
+def finish_kernel(
+    out,
+    input_grad,
+    along,
+    grad_a,
+    grad_i,
+    grad_d,
+    sums,
+    out_o,
+    input_grad_o,
+    along_o,
+    grad_qkv_o,
+    grad_out_o,
+    grad_i_o,
+    grad_d_o,
+    grad_gains_o,
+    grad_shifts_o,
+    grad_in_bias_o,
+    grad_qvb_o,
+):
+    out_o[...] = out[...]
+    input_grad_o[...] = input_grad[...].astype(F32)
+    along_o[...] = along[...].astype(F32)
+
+    @pl.when(pl.program_id(0) == 0)
+    def _():
+        dp = lax.axis_index("dp")
+        mp = lax.axis_index("mp")
+        rows, width = grad_a.shape
+        head_cols = grad_out_o.shape[0]
+        exact = lax.Precision.HIGHEST
+
+        def pick(values, share, offset):
+            places = one_hot(share, width, offset, F32)
+            return lax.dot_general(
+                values,
+                places,
+                (((1,), (1,)), ((), ())),
+                precision=exact,
+                preferred_element_type=F32,
+            )
+
+        for part in range(3):
+            grad_qkv_o[part] = grad_a[:, part * head_cols : (part + 1) * head_cols]
+        grad_out_o[...] = lax.dot_general(
+            grad_a[:, 3 * head_cols :],
+            one_hot(rows, rows, 0, F32),
+            (((0,), (0,)), ((), ())),
+            precision=exact,
+            preferred_element_type=F32,
+        )
+        grad_i_o[...] = grad_i[...]
+        grad_d_o[...] = grad_d[...]
+        share = grad_gains_o.shape[1]
+        bias_share = grad_qvb_o.shape[1]
+        norms = pick(sums[0:8, :], share, dp * share)
+        grad_gains_o[...] = norms[0:2]
+        grad_shifts_o[...] = norms[2:6]
+        grad_in_bias_o[...] = pick(sums[pl.ds(BIAS_ROW + mp, 1), :], share, dp * share)
+        row = sums[pl.ds(QKV_ROW + mp, 1), :]
+        grad_qvb_o[0:1, :] = pick(row, bias_share, dp * bias_share)
+        grad_qvb_o[1:2, :] = pick(row, bias_share, 2 * head_cols + dp * bias_share)
+
+
+def run_finish(
+    out, input_grad, along, grad_a, grad_i, grad_d, sums, head_cols, share, bias_share
+):
+    steps = 4
+    rows, width = out.shape
+    local_rows = grad_a.shape[0]
+
+    def whole(*shape):
+        return pl.BlockSpec(shape, lambda i: (0,) * len(shape))
+
+    slab = pl.BlockSpec((rows // steps, width), lambda i: (i, 0))
+    shapes = (
+        (3, local_rows, head_cols),
+        (head_cols, local_rows),
+        (local_rows, width),
+        (local_rows, width),
+        (2, share),
+        (4, share),
+        (1, share),
+        (2, bias_share),
+    )
+    return pl.pallas_call(
+        finish_kernel,
+        grid=(steps,),
+        out_shape=(
+            jax.ShapeDtypeStruct(out.shape, BF16),
+            jax.ShapeDtypeStruct(out.shape, F32),
+            jax.ShapeDtypeStruct(out.shape, F32),
+        )
+        + tuple(jax.ShapeDtypeStruct(shape, F32) for shape in shapes),
+        in_specs=[slab] * 3 + [whole(local_rows, width)] * 3 + [whole(*sums.shape)],
+        out_specs=(slab,) * 3 + tuple(whole(*shape) for shape in shapes),
+        name="finish",
+    )(out, input_grad, along, grad_a, grad_i, grad_d, sums)
 
 
 def local(
@@ -767,54 +890,22 @@
     n_dp = lax.axis_size("dp")
     inner = n_dp // BLOCKS
     groups = [[b * inner + i for i in range(inner)] for b in range(BLOCKS)]
-    dp = lax.axis_index("dp")
-    mp = lax.axis_index("mp")
-    width = tokens.shape[1]
     head_cols = w_out.shape[0]
     local_rows = w_qkv.shape[0]
-    shards = (
-        jnp.concatenate([w_qkv.reshape(local_rows, 3 * head_cols), w_out.T], 1),
-        w_in,
-        w_down.T,
-        pilot.T,
-    )
-
-    spot = jnp.arange(width, dtype=jnp.int32)
-    share = gains.shape[1]
-
-    def spread(values, period, offset):
-        per = values.shape[1]
-        tiled = jnp.tile(values, (1, period // per))
-        tiled = jnp.pad(tiled, ((0, 0), (offset, width - offset - period)))
-        place = (spot - offset) // per == dp
-        return jnp.where(place & (spot >= offset) & (spot < offset + period), tiled, 0)
-
-    head = (mp == 0).astype(F32)
-    vectors = spread(jnp.concatenate([gains, shifts], 0).astype(F32), width, 0) * head
-    at_mp = (jnp.arange(GROUP) == mp).astype(F32)[:, None]
-    hidden_bias = spread(in_bias.astype(F32), width, 0) * at_mp
-    pair = qv_bias.reshape(2, -1).astype(F32)
-    qkv_bias = (
-        spread(pair[0:1], head_cols, 0) + spread(pair[1:2], head_cols, 2 * head_cols)
-    ) * at_mp
-    small = jnp.concatenate(
-        [
-            vectors,
-            hidden_bias,
-            qkv_bias,
-            jnp.zeros((SMALL_ROWS - QKV_ROW - GROUP, width), F32),
-        ],
-        0,
-    )
+    shards = (w_in, w_down.T, pilot.T)
+    projections = (w_qkv.transpose(1, 0, 2), w_out)
+    small = (gains, shifts, in_bias, qv_bias.reshape(2, -1))
     if inner > 1:
-        shards = tuple(
-            lax.all_gather(item, "dp", axis=0, tiled=True, axis_index_groups=groups)
-            for item in shards
-        )
-        small = lax.psum(small, "dp", axis_index_groups=groups)
+
+        def joined(item, axis):
+            return lax.all_gather(item, "dp", axis=axis, tiled=True, axis_index_groups=groups)
+
+        shards = tuple(joined(item, 0) for item in shards)
+        projections = tuple(joined(item, 1) for item in projections)
+        small = tuple(joined(item, 1) for item in small)
 
     out, along, input_grad, grad_a, grad_i, grad_d, sums = run_layer(
-        inner, lengths, tokens, cotangent, shards, small
+        inner, lengths, tokens, cotangent, shards, projections, small
     )
     if inner > 1:
         grad_a, grad_i, grad_d = (
@@ -824,30 +915,33 @@
             for item in (grad_a, grad_i, grad_d)
         )
         sums = lax.psum(sums, "dp", axis_index_groups=groups)
-
-    columns = lax.dynamic_slice_in_dim(sums, dp * share, share, 1)
-    bias_share = qv_bias.shape[2]
-    bias_row = lax.dynamic_slice_in_dim(sums, QKV_ROW + mp, 1, 0)
-    grad_qvb = jnp.stack(
-        [
-            lax.dynamic_slice_in_dim(bias_row, dp * bias_share, bias_share, 1),
-            lax.dynamic_slice_in_dim(
-                bias_row, 2 * head_cols + dp * bias_share, bias_share, 1
-            ),
-        ]
+    (
+        out,
+        input_grad,
+        along,
+        grad_qkv,
+        grad_out,
+        grad_i,
+        grad_d,
+        grad_gains,
+        grad_shifts,
+        grad_in_bias,
+        grad_qvb,
+    ) = run_finish(
+        out, input_grad, along, grad_a, grad_i, grad_d, sums, head_cols, gains.shape[1], qv_bias.shape[2]
     )
     return (
         out,
-        input_grad.astype(F32),
-        along.astype(F32),
-        grad_a[:, : 3 * head_cols].reshape(local_rows, 3, head_cols),
-        grad_qvb,
-        grad_a[:, 3 * head_cols :].T,
+        input_grad,
+        along,
+        grad_qkv.transpose(1, 0, 2),
+        grad_qvb.reshape(qv_bias.shape),
+        grad_out,
         grad_i,
-        lax.dynamic_slice_in_dim(columns, BIAS_ROW + mp, 1, 0),
+        grad_in_bias,
         grad_d.T,
-        columns[0:2],
-        columns[2:6],
+        grad_gains,
+        grad_shifts,
     )
 
 

time: 189 us -> 175 us (0.926)
  local copies, waits for them, and re-layouts: 11.7 us -> 0 us
  other arithmetic: 9.48 us -> 0 us
  Pallas kernels: 166 us -> 173 us
    pallas_call x0 -> x1, Pallas kernels: none -> 7.49 us  [run_finish(): pl.pallas_call(finish_kernel, grid=(steps,), out_shape=(jax.ShapeDtypeStr...]
    convert_element_type x5 -> x0, other arithmetic: 6.67 us -> none  [the longest x1 3.42 us: local(): input_grad.astype(F32)]
    unnamed x17 -> x0, local copies, waits for them, and re-layouts: 6.17 us -> none
    slice x4 -> x0, local copies, waits for them, and re-layouts: 2.84 us -> none  [the longest x1 1.35 us: local(): columns[2:6]]
where the time goes in v5:
time: 175 us; the launch traced here: 174 us
  Pallas kernels  173 us (99%)
    pallas_call x1, Pallas kernels, run_layer(): pl.pallas_call(functools.partial(layer_kernel, inner), out_shape=(whole,...  166 us
    pallas_call x1, Pallas kernels, run_finish(): pl.pallas_call(finish_kernel, grid=(steps,), out_shape=(jax.ShapeDtypeStr...  7.49 us

profile of v5, /device:TPU:25, one launch (start us, length us, event | category | flops | bytes accessed | tf_op | source)
XLA Modules:
  0.0 174.1 jit_solution(8046682692278736892)
XLA Ops:
  0.6 165.8 %layer.1 = (bf16[1024,768]{1,0:T(8,128)(2,1)}, bf16[1024,768]{1,0:T(8,128)(2,1)}, bf16[1024,768]{1,0:T(8,128)(2,1)}, f32[96,768]{1,0:T(8,128)}, f32[96,768]{1,0:...) custom-call(s32[4]{0:T(128)} %lens.1, bf16[1024,768]{1,0:T(8,128)(2,1)} %tok.1, bf16[1024,768]{1,0:T(8,128)(2,1)} %cot.1, ...), custom_call_target="tpu_custom_call" | custom-call | tf_op jit(solution)/shard_map/layer/pallas_call | solution.py:766
  166.5 7.5 %finish.1 = (bf16[1024,768]{1,0:T(8,128)(2,1)}, f32[1024,768]{1,0:T(8,128)}, f32[1024,768]{1,0:T(8,128)}, f32[3,96,192]{2,1,0:T(8,128)}, f32[192,96]{1,0:T(8,128...) custom-call(bf16[1024,768]{1,0:T(8,128)(2,1)} %get-tuple-element.29., ...), custom_call_target="tpu_custom_call" | custom-call | tf_op jit(solution)/shard_map/finish/pallas_call | solution.py:872

commit v6 on v5

--- a/solution.py
+++ b/solution.py
@@ -19,6 +19,7 @@
 QKV_ROW = BIAS_ROW + GROUP
 FWD_ROWS = 48
 BWD_ROWS = 48
+DEEP_ROWS = 32
 F32 = jnp.float32
 BF16 = jnp.bfloat16
 QKV, IN, DOWN, PILOT = range(4)
@@ -83,6 +84,8 @@
     r_xs,
     r_ys,
     r_z,
+    r_deep,
+    r_plane,
     par,
     par_in,
     gs,
@@ -125,6 +128,10 @@
     r_red,
     s_rz,
     r_rz,
+    s_deep,
+    r_deeps,
+    s_plane,
+    r_planes,
     s_sm,
     r_sm,
     s_out,
@@ -153,6 +160,7 @@
     x_peer = {"dp": (z * NX + far_x) * inner + rest, "mp": mp}
     y_peer = {"dp": dp, "mp": over_y}
     c_peer = {"dp": dp, "mp": y * NC + far_c}
+    corner_peer = {"dp": x_peer["dp"], "mp": over_y}
 
     def z_at(step):
         return (z + step) % NZ
@@ -184,7 +192,7 @@
         remote(dst, dst, send, recv, c_peer).wait_recv()
 
     barrier = pltpu.get_barrier_semaphore()
-    peers = [x_peer, y_peer, c_peer] + [z_peer(step) for step in range(1, NZ)]
+    peers = [x_peer, y_peer, c_peer, corner_peer] + [z_peer(step) for step in range(1, NZ)]
     for peer in peers:
         pl.semaphore_signal(barrier, inc=1, device_id=peer, device_id_type=pl.DeviceIdType.MESH)
 
@@ -293,10 +301,12 @@
                 s_dx.at[k, step],
                 r_dx.at[k, step],
             )
-        exchange_core(k)
 
     def exchange_core(k):
         to_core(k, 3, over_y, far_x)
+        from_core(k)
+
+    def from_core(k):
         for index, (block_index, column) in enumerate(
             (
                 (y * NC + far_c, x),
@@ -372,6 +382,7 @@
     send_z(DOWN)
     par[4] = small_last(0, par, par_in)
     finish(QKV)
+    exchange_core(QKV)
 
     length = lens[mp]
     key_keep = lax.broadcasted_iota(jnp.int32, (rows, rows), 1) < length
@@ -409,13 +420,14 @@
     forward_diagonal(IN, 3)
     forward_z(DOWN, 1)
     forward_diagonal(PILOT, 0)
+    send_z(PILOT)
+    side_z(PILOT)
     lax.fori_loop(0, NY, attend, 0)
     forward_diagonal(IN, 2)
     columns_to_core(IN)
     forward_z(DOWN, 3)
-    send_z(PILOT)
-    side_z(PILOT)
     forward_diagonal(DOWN, 0)
+    corner_z(PILOT)
     lax.fori_loop(NY, GROUP, attend, 0)
 
     acc[...] = jnp.zeros_like(acc)
@@ -437,8 +449,8 @@
     to_core(DOWN, 0, mine, x)
     forward_diagonal(DOWN, 1)
     finish(IN)
+    exchange_core(IN)
     forward_diagonal(DOWN, 3)
-    corner_z(PILOT)
 
     def expand(m, carry):
         pre = nn(low[...], square(w_i, m, 0, width)) + par[4, pl.ds(BIAS_ROW + m, 1), :]
@@ -451,15 +463,18 @@
     low_t[...] = low[...].T
     forward_diagonal(DOWN, 2)
     columns_to_core(DOWN)
+    acc[...] = xh1[...] * par_row(0) + par_row(3) + par_row(4)
+
+    def contract(m):
+        acc[...] += nt(hid[m], square(w_d, m, 0, width))
+
+    contract(mine)
     finish(DOWN)
-
-    acc[...] = xh1[...] * par_row(0) + par_row(3) + par_row(4)
-
-    def contract(m, carry):
-        acc[...] += nt(hid[m], square(w_d, m, 0, width))
-        return carry
-
-    lax.fori_loop(0, GROUP, contract, 0)
+    to_core(DOWN, 3, over_y, far_x)
+    contract(over_y)
+    from_core(DOWN)
+    contract(y * NC + far_c)
+    contract(far_y * NC + far_c)
     stream = acc[...]
     centered = stream - row_mean(stream)
     rstd = lax.rsqrt(row_mean(centered * centered) + EPSILON)
@@ -540,74 +555,154 @@
             to_partner(g_i, 1, i).start()
 
 
-    top_rows = pl.ds(0, BWD_ROWS)
-    low_rows = pl.ds(BWD_ROWS, block - BWD_ROWS)
+    def flat_rows(k):
+        return block - DEEP_ROWS if k == 0 else block
+
+    def half_rows(k):
+        return (block - DEEP_ROWS) // 2 if k == 0 else BWD_ROWS
+
+    def top_rows(k):
+        return pl.ds(0, half_rows(k))
+
+    def low_rows(k):
+        return pl.ds(half_rows(k), flat_rows(k) - half_rows(k))
+
+    def low_part(k):
+        return pl.ds(0, flat_rows(k) - half_rows(k))
+
+    deep = pl.ds(block - DEEP_ROWS, DEEP_ROWS)
+
+    def deep_first(ref):
+        for step in range(1, NZ):
+            for index, m in enumerate((mine, over_y)):
+                push(
+                    ref.at[m, z_at(step), :, deep],
+                    r_deep.at[step - 1, index],
+                    s_deep.at[step, index],
+                    r_deeps.at[step, index],
+                    z_peer(step),
+                )
+
+    def deep_second(ref):
+        for index, m in enumerate((mine, over_y)):
+            total = ref[m, z, :, deep, :].astype(F32)
+            for step in range(1, NZ):
+                arrived(r_deep.at[step - 1, index], s_deep.at[step, index], r_deeps.at[step, index])
+                total = total + r_deep[step - 1, index].astype(F32)
+            ref[m, z, :, deep, :] = total.astype(BF16)
+        for index, (m, column, peer) in enumerate(
+            ((over_y, x, y_peer), (mine, far_x, x_peer), (over_y, far_x, corner_peer))
+        ):
+            push(
+                ref.at[m, z, column, deep],
+                r_plane.at[index],
+                s_plane.at[index],
+                r_planes.at[index],
+                peer,
+            )
+
+    def add_core_block(k, ref, yy):
+        m = yy * NC + c
+        remote(
+            ref.at[m], r_core.at[k, yy], s_rc.at[k, yy], r_rc.at[k, yy], c_peer
+        ).wait_recv()
+
+        def one(zz, carry):
+            ref[m, zz] = ref[m, zz] + r_core[k, yy, zz]
+            return carry
+
+        lax.fori_loop(0, NZ, one, 0)
+
+    def first_over_y(k, ref):
+        push(
+            ref.at[over_y, :, :, top_rows(k)],
+            r_yf.at[k, :, :, top_rows(k)],
+            s_red.at[k, 0],
+            r_red.at[k, 0],
+            y_peer,
+        )
+
+    def first_over_x(k, ref, yy):
+        push(
+            ref.at[yy * NC + c, :, far_x, low_rows(k)],
+            r_xf.at[k, yy, :, low_part(k)],
+            s_red.at[k, 1 + yy],
+            r_red.at[k, 1 + yy],
+            x_peer,
+        )
 
     def add_core(k, ref):
         for yy in range(NY):
-            m = yy * NC + c
-            to_partner(ref, k, yy).wait_recv()
-
-            def one(zz, carry):
-                ref[m, zz] = ref[m, zz] + r_core[k, yy, zz]
-                return carry
-
-            lax.fori_loop(0, NZ, one, 0)
+            add_core_block(k, ref, yy)
 
     def reduce_first(k, ref):
+        first_over_y(k, ref)
+        for yy in range(NY):
+            first_over_x(k, ref, yy)
+
+    def reduce_second(k, ref):
+        top, low, part = top_rows(k), low_rows(k), low_part(k)
+        arrived(r_yf.at[k, :, :, top], s_red.at[k, 0], r_red.at[k, 0])
+        ref[mine, :, :, top, :] = ref[mine, :, :, top, :] + r_yf[k, :, :, top, :]
         push(
-            ref.at[over_y, :, :, top_rows], r_yf.at[k], s_red.at[k, 0], r_red.at[k, 0], y_peer
-        )
-        for yy in range(NY):
-            push(
-                ref.at[yy * NC + c, :, far_x, low_rows],
-                r_xf.at[k, yy],
-                s_red.at[k, 1 + yy],
-                r_red.at[k, 1 + yy],
-                x_peer,
-            )
-
-    def reduce_second(k, ref):
-        arrived(r_yf.at[k], s_red.at[k, 0], r_red.at[k, 0])
-        ref[mine, :, :, top_rows, :] = ref[mine, :, :, top_rows, :] + r_yf[k]
-        push(
-            ref.at[mine, :, far_x, top_rows], r_xs.at[k], s_red.at[k, 3], r_red.at[k, 3], x_peer
+            ref.at[mine, :, far_x, top],
+            r_xs.at[k, :, top],
+            s_red.at[k, 3],
+            r_red.at[k, 3],
+            x_peer,
         )
         for yy in range(NY):
             m = yy * NC + c
-            arrived(r_xf.at[k, yy], s_red.at[k, 1 + yy], r_red.at[k, 1 + yy])
-            ref[m, :, x, low_rows, :] = ref[m, :, x, low_rows, :] + r_xf[k, yy]
+            arrived(r_xf.at[k, yy, :, part], s_red.at[k, 1 + yy], r_red.at[k, 1 + yy])
+            ref[m, :, x, low, :] = ref[m, :, x, low, :] + r_xf[k, yy, :, part, :]
         push(
-            ref.at[over_y, :, x, low_rows], r_ys.at[k], s_red.at[k, 4], r_red.at[k, 4], y_peer
+            ref.at[over_y, :, x, low],
+            r_ys.at[k, :, part],
+            s_red.at[k, 4],
+            r_red.at[k, 4],
+            y_peer,
         )
 
     def reduce_third(k, ref):
-        arrived(r_xs.at[k], s_red.at[k, 3], r_red.at[k, 3])
-        ref[mine, :, x, top_rows, :] = ref[mine, :, x, top_rows, :] + r_xs[k]
-        arrived(r_ys.at[k], s_red.at[k, 4], r_red.at[k, 4])
-        ref[mine, :, x, low_rows, :] = ref[mine, :, x, low_rows, :] + r_ys[k]
+        top, low, part = top_rows(k), low_rows(k), low_part(k)
+        arrived(r_xs.at[k, :, top], s_red.at[k, 3], r_red.at[k, 3])
+        ref[mine, :, x, top, :] = ref[mine, :, x, top, :] + r_xs[k, :, top, :]
+        arrived(r_ys.at[k, :, part], s_red.at[k, 4], r_red.at[k, 4])
+        ref[mine, :, x, low, :] = ref[mine, :, x, low, :] + r_ys[k, :, part, :]
+        flat = pl.ds(0, flat_rows(k))
         for step in range(1, NZ):
             push(
-                ref.at[mine, z_at(step), x],
-                r_z.at[k, step - 1],
+                ref.at[mine, z_at(step), x, flat],
+                r_z.at[k, step - 1, flat],
                 s_rz.at[k, step],
                 r_rz.at[k, step],
                 z_peer(step),
             )
 
     def reduce_last(k, ref, result):
-        total = ref[mine, z, x].astype(F32)
+        flat = pl.ds(0, flat_rows(k))
+        total = ref[mine, z, x, flat, :].astype(F32)
         for step in range(1, NZ):
-            arrived(r_z.at[k, step - 1], s_rz.at[k, step], r_rz.at[k, step])
-            total = total + r_z[k, step - 1].astype(F32)
-        result[...] = total
-
-    for i in range(GROUP):
+            arrived(r_z.at[k, step - 1, flat], s_rz.at[k, step], r_rz.at[k, step])
+            total = total + r_z[k, step - 1, flat, :].astype(F32)
+        result[flat, :] = total
+        if k == 0:
+            total = ref[mine, z, x, deep, :].astype(F32)
+            for index in range(3):
+                arrived(r_plane.at[index], s_plane.at[index], r_planes.at[index])
+                total = total + r_plane[index].astype(F32)
+            result[deep, :] = total
+
+    for i in range(NY):
         outer(bl_t, hid.at[block_of(i)], g_d, block_of(i), 0, width)
-        if i < NY:
-            to_partner(g_d, 0, i).start()
-    add_core(0, g_d)
-    reduce_first(0, g_d)
+        to_partner(g_d, 0, i).start()
+    for yy in (far_y, y):
+        outer(bl_t, hid.at[yy * NC + c], g_d, yy * NC + c, 0, width)
+        add_core_block(0, g_d, yy)
+        first_over_x(0, g_d, yy)
+        if yy is far_y:
+            first_over_y(0, g_d)
+    deep_first(g_d)
     for i in range(GROUP):
         back_ff(i)
     add_core(1, g_i)
@@ -666,6 +761,7 @@
     reduce_first(2, g_a)
     small_add(1, gs, gs_in, 0)
     small_stage(1, gs, gs_in, 1)
+    deep_second(g_d)
     reduce_third(0, g_d)
     finish_z(PILOT)
     acc[...] = jnp.zeros_like(acc)
@@ -728,6 +824,8 @@
             pltpu.VMEM((grads, NZ, BWD_ROWS, width), BF16),
             pltpu.VMEM((grads, NZ, block - BWD_ROWS, width), BF16),
             pltpu.VMEM((grads, NZ - 1, block, width), BF16),
+            pltpu.VMEM((NZ - 1, 2, NX, DEEP_ROWS, width), BF16),
+            pltpu.VMEM((3, DEEP_ROWS, width), BF16),
             pltpu.VMEM((5, SMALL_ROWS, width), F32),
             pltpu.VMEM((6, SMALL_ROWS, width), F32),
             pltpu.VMEM((4, SMALL_ROWS, width), F32),
@@ -757,6 +855,8 @@
         + [dma((grads, NY))] * 2
         + [dma((grads, 5))] * 2
         + [dma((grads, NZ))] * 2
+        + [dma((NZ, 2))] * 2
+        + [dma((3,))] * 2
         + [dma((2, 6))] * 2
         + [dma((3, 3))] * 2
         + [dma((3,))]
@@ -851,7 +951,7 @@
 def run_finish(
     out, input_grad, along, grad_a, grad_i, grad_d, sums, head_cols, share, bias_share
 ):
-    steps = 4
+    steps = 2
     rows, width = out.shape
     local_rows = grad_a.shape[0]
 

time: 175 us -> 170 us (0.971)
  Pallas kernels: 173 us -> 169 us
    pallas_call x1, Pallas kernels: 166 us -> 162 us  [run_layer(): pl.pallas_call(functools.partial(layer_kernel, inner), out_shape=(whole,...]
where the time goes in v6:
time: 170 us; the launch traced here: 169 us
  Pallas kernels  169 us (99%)
    pallas_call x1, Pallas kernels, run_layer(): pl.pallas_call(functools.partial(layer_kernel, inner), out_shape=(whole,...  162 us
    pallas_call x1, Pallas kernels, run_finish(): pl.pallas_call(finish_kernel, grid=(steps,), out_shape=(jax.ShapeDtypeStr...  6.77 us

profile of v6, /device:TPU:25, one launch (start us, length us, event | category | flops | bytes accessed | tf_op | source)
XLA Modules:
  0.0 169.4 jit_solution(9740603202645565273)
XLA Ops:
  0.6 161.9 %layer.1 = (bf16[1024,768]{1,0:T(8,128)(2,1)}, bf16[1024,768]{1,0:T(8,128)(2,1)}, bf16[1024,768]{1,0:T(8,128)(2,1)}, f32[96,768]{1,0:T(8,128)}, f32[96,768]{1,0:...) custom-call(s32[4]{0:T(128)} %lens.1, bf16[1024,768]{1,0:T(8,128)(2,1)} %tok.1, bf16[1024,768]{1,0:T(8,128)(2,1)} %cot.1, ...), custom_call_target="tpu_custom_call" | custom-call | tf_op jit(solution)/shard_map/layer/pallas_call | solution.py:866
  162.5 6.8 %finish.1 = (bf16[1024,768]{1,0:T(8,128)(2,1)}, f32[1024,768]{1,0:T(8,128)}, f32[1024,768]{1,0:T(8,128)}, f32[3,96,192]{2,1,0:T(8,128)}, f32[192,96]{1,0:T(8,128...) custom-call(bf16[1024,768]{1,0:T(8,128)(2,1)} %get-tuple-element.29., ...), custom_call_target="tpu_custom_call" | custom-call | tf_op jit(solution)/shard_map/finish/pallas_call | solution.py:972

commit v7 on v6

--- a/solution.py
+++ b/solution.py
@@ -163,10 +163,15 @@
     corner_peer = {"dp": x_peer["dp"], "mp": over_y}
 
     def z_at(step):
-        return (z + step) % NZ
-
-    def z_from(step):
-        return (z + NZ - step) % NZ
+        if step == 0:
+            return z
+        if step == 1:
+            return z + 1 - 2 * (z % 2)
+        if step == 2:
+            return (z + NZ // 2) % NZ
+        return NZ - 1 - z
+
+    z_from = z_at
 
     def z_peer(step):
         return {"dp": (z_at(step) * NX + x) * inner + rest, "mp": mp}
@@ -223,7 +228,7 @@
     loads.append(pltpu.make_async_copy(cot.at[my_rows], cots, s_load.at[5]))
 
     def send_z(k):
-        for step in range(1, NZ):
+        for step in (1, 2):
             push(
                 shards[k],
                 weights[k].at[mine, z, x],
@@ -240,6 +245,8 @@
     def forward_z(k, step):
         src = weights[k].at[mine, z_from(step), x]
         arrived(src, s_z.at[k, step], r_zs.at[k, step])
+        if step == 2:
+            push(src, src, s_z.at[k, 3], r_zs.at[k, 3], z_peer(1), k)
         push(src, src, s_x.at[k, step], r_x.at[k, step], x_peer, k)
         push(src, src, s_y.at[k, step], r_y.at[k, step], y_peer, k)
 
@@ -261,21 +268,40 @@
         push(src, src, s_c.at[k, index], r_c.at[k, index], c_peer, k)
 
     def side_z(k):
-        for step in range(1, NZ):
+        arrived(weights[k].at[mine, z, far_x], s_x.at[k, 0], r_x.at[k, 0])
+        arrived(weights[k].at[over_y, z, x], s_y.at[k, 0], r_y.at[k, 0])
+        for step in (1, 2):
             src = weights[k].at[mine, z, far_x]
             push(src, src, s_x.at[k, step], r_x.at[k, step], z_peer(step), k)
             src = weights[k].at[over_y, z, x]
             push(src, src, s_y.at[k, step], r_y.at[k, step], z_peer(step), k)
 
+    def corner_x(k):
+        src = weights[k].at[over_y, z, x]
+        push(src, src, s_dx.at[k, 0], r_dx.at[k, 0], x_peer, k)
+
     def corner_z(k):
-        arrived(weights[k].at[over_y, z, far_x, first], s_dy.at[k, 0], r_dy.at[k, 0])
-        arrived(weights[k].at[over_y, z, far_x, second], s_dx.at[k, 0], r_dx.at[k, 0])
         src = weights[k].at[over_y, z, far_x]
-        for step in range(1, NZ):
+        arrived(src, s_dx.at[k, 0], r_dx.at[k, 0])
+        for step in (1, 2):
             push(src, src, s_dx.at[k, step], r_dx.at[k, step], z_peer(step), k)
 
+    def side_relay(k):
+        for src, send, recv in (
+            (weights[k].at[mine, z_from(2), x], s_z, r_zs),
+            (weights[k].at[mine, z_from(2), far_x], s_x, r_x),
+            (weights[k].at[over_y, z_from(2), x], s_y, r_y),
+        ):
+            arrived(src, send.at[k, 2], recv.at[k, 2])
+            push(src, src, send.at[k, 3], recv.at[k, 3], z_peer(1), k)
+
+    def corner_relay(k):
+        src = weights[k].at[over_y, z_from(2), far_x]
+        arrived(src, s_dx.at[k, 2], r_dx.at[k, 2])
+        push(src, src, s_dx.at[k, 3], r_dx.at[k, 3], z_peer(1), k)
+
     def finish_z(k):
-        for step in range(1, NZ):
+        for step in (1, 3):
             at = z_from(step)
             arrived(weights[k].at[mine, at, x], s_z.at[k, step], r_zs.at[k, step])
             arrived(weights[k].at[mine, at, far_x], s_x.at[k, step], r_x.at[k, step])
@@ -362,24 +388,24 @@
     small_stage(0, par, par_in, 2)
     send_own(PILOT)
     forward_diagonal(QKV, 0)
-    forward_z(QKV, 3)
+    forward_z(QKV, 2)
+    send_z(IN)
     small_add(0, par, par_in, 2)
     small_stage(0, par, par_in, 3)
     forward_diagonal(QKV, 1)
-    forward_z(QKV, 2)
-    send_z(IN)
+    forward_z(QKV, 3)
     for copy in loads:
         copy.wait()
     to_core(QKV, 0, mine, x)
+    forward_diagonal(QKV, 2)
+    forward_z(IN, 1)
     forward_diagonal(QKV, 3)
-    forward_z(IN, 1)
-    forward_diagonal(QKV, 2)
     columns_to_core(QKV)
+    forward_z(IN, 2)
+    send_z(DOWN)
+    forward_diagonal(IN, 0)
     forward_z(IN, 3)
-    forward_diagonal(IN, 0)
-    forward_z(IN, 2)
     to_core(IN, 0, mine, x)
-    send_z(DOWN)
     par[4] = small_last(0, par, par_in)
     finish(QKV)
     exchange_core(QKV)
@@ -417,17 +443,15 @@
         return carry
 
     forward_diagonal(IN, 1)
+    forward_diagonal(IN, 2)
+    forward_z(DOWN, 1)
+    lax.fori_loop(0, NY, attend, 0)
     forward_diagonal(IN, 3)
-    forward_z(DOWN, 1)
-    forward_diagonal(PILOT, 0)
+    columns_to_core(IN)
+    forward_z(DOWN, 2)
     send_z(PILOT)
     side_z(PILOT)
-    lax.fori_loop(0, NY, attend, 0)
-    forward_diagonal(IN, 2)
-    columns_to_core(IN)
-    forward_z(DOWN, 3)
     forward_diagonal(DOWN, 0)
-    corner_z(PILOT)
     lax.fori_loop(NY, GROUP, attend, 0)
 
     acc[...] = jnp.zeros_like(acc)
@@ -445,12 +469,12 @@
     xh1[...] = xhat
     normed_low = (xhat * par_row(0) + par_row(3)).astype(BF16)
     low[...] = normed_low
-    forward_z(DOWN, 2)
+    forward_z(DOWN, 3)
     to_core(DOWN, 0, mine, x)
     forward_diagonal(DOWN, 1)
     finish(IN)
     exchange_core(IN)
-    forward_diagonal(DOWN, 3)
+    forward_diagonal(DOWN, 2)
 
     def expand(m, carry):
         pre = nn(low[...], square(w_i, m, 0, width)) + par[4, pl.ds(BIAS_ROW + m, 1), :]
@@ -461,7 +485,7 @@
 
     lax.fori_loop(0, GROUP, expand, 0)
     low_t[...] = low[...].T
-    forward_diagonal(DOWN, 2)
+    forward_diagonal(DOWN, 3)
     columns_to_core(DOWN)
     acc[...] = xh1[...] * par_row(0) + par_row(3) + par_row(4)
 
@@ -471,6 +495,7 @@
     contract(mine)
     finish(DOWN)
     to_core(DOWN, 3, over_y, far_x)
+    corner_x(PILOT)
     contract(over_y)
     from_core(DOWN)
     contract(y * NC + far_c)
@@ -696,6 +721,8 @@
     for i in range(NY):
         outer(bl_t, hid.at[block_of(i)], g_d, block_of(i), 0, width)
         to_partner(g_d, 0, i).start()
+    corner_z(PILOT)
+    side_relay(PILOT)
     for yy in (far_y, y):
         outer(bl_t, hid.at[yy * NC + c], g_d, yy * NC + c, 0, width)
         add_core_block(0, g_d, yy)
@@ -752,6 +779,8 @@
             copy.wait_send()
     for i in range(GROUP):
         back_attention(i)
+        if i == 0:
+            corner_relay(PILOT)
         if i == 2:
             reduce_second(0, g_d)
     own[2] = acc[...].astype(BF16)

time: 170 us -> 168 us (0.988); the launches traced: 169 us -> 164 us
  Pallas kernels: 169 us -> 164 us
    pallas_call x1, Pallas kernels: 162 us -> 157 us  [run_layer(): pl.pallas_call(functools.partial(layer_kernel, inner), out_shape=(whole,...]
where the time goes in v7:
time: 168 us; the launch traced here: 164 us
  Pallas kernels  164 us (98%)
    pallas_call x1, Pallas kernels, run_layer(): pl.pallas_call(functools.partial(layer_kernel, inner), out_shape=(whole,...  157 us
    pallas_call x1, Pallas kernels, run_finish(): pl.pallas_call(finish_kernel, grid=(steps,), out_shape=(jax.ShapeDtypeStr...  6.77 us

profile of v7, /device:TPU:25, one launch (start us, length us, event | category | flops | bytes accessed | tf_op | source)
XLA Modules:
  0.0 164.4 jit_solution(16015543996393071496)
XLA Ops:
  0.6 156.9 %layer.1 = (bf16[1024,768]{1,0:T(8,128)(2,1)}, bf16[1024,768]{1,0:T(8,128)(2,1)}, bf16[1024,768]{1,0:T(8,128)(2,1)}, f32[96,768]{1,0:T(8,128)}, f32[96,768]{1,0:...) custom-call(s32[4]{0:T(128)} %lens.1, bf16[1024,768]{1,0:T(8,128)(2,1)} %tok.1, bf16[1024,768]{1,0:T(8,128)(2,1)} %cot.1, ...), custom_call_target="tpu_custom_call" | custom-call | tf_op jit(solution)/shard_map/layer/pallas_call | solution.py:895
  157.5 6.8 %finish.1 = (bf16[1024,768]{1,0:T(8,128)(2,1)}, f32[1024,768]{1,0:T(8,128)}, f32[1024,768]{1,0:T(8,128)}, f32[3,96,192]{2,1,0:T(8,128)}, f32[192,96]{1,0:T(8,128...) custom-call(bf16[1024,768]{1,0:T(8,128)(2,1)} %get-tuple-element.29., ...), custom_call_target="tpu_custom_call" | custom-call | tf_op jit(solution)/shard_map/finish/pallas_call | solution.py:1001
